TPU v7x, 32 devices: a whole 2x2x4 slice. The times are simulated.
32 devices in a mesh: groups: 2 (over y), rows: 4 (over z), clips: 2 (over x), frames: 2 (over core).
Axes of the slice: x: 2, y: 2, z: 4, core: 2. Of those that a mesh axis runs over, the one named last changes fastest.
Arguments:
- pixels: bfloat16 [4, 8, 3, 16, 256], P(('groups', 'clips'), 'frames', None, 'rows'), parts along dimension 0, may hold values from -6 to 6
- frame_counts: int32 [4], P(('groups', 'clips')), parts along dimension 0, may hold values from 1 to 8
- weight_first: bfloat16 [3, 3, 3, 64, 3], replicated, may hold values from -0.625 to 0.625
- weight_second: bfloat16 [3, 3, 3, 64, 64], replicated, may hold values from -0.15625 to 0.15625
- weight_down: bfloat16 [3, 3, 64, 64], replicated, may hold values from -0.25 to 0.25
Outputs:
- encoded: bfloat16 [4, 8, 64, 8, 128], P(('groups', 'clips'), 'frames', None, 'rows'), parts along dimension 0
There are 2 independent parts, one for each index of `groups`. A program takes and returns all parts, laid end to end along the dimension named above; an argument that names none is the same for every part. Nothing has to cross between parts.
Inputs may be any that keep to these rules, and one draw needn't show every extreme that they name: `frame_counts`: the number of real frames of each clip; later frame slots are ignored.
All inputs are finite; a program needn't handle non-finite values.
Results may differ from a plain program's by a relative error of at most 0.006.
Values may be sent and summed in bfloat16 or wider, within the bound.
No kernel may reach another device: no remote copies, remote signals or barrier semaphores. Data moves between devices by JAX's collectives and lax.ppermute only.
A program may use at most 64 MiB of HBM per device.

v0:
```python
import jax
import jax.numpy as jnp
from jax import lax
from jax.sharding import PartitionSpec as P


def passed_along(block, axis, distance):
    devices = range(lax.axis_size(axis))
    route = [(i - distance, i) for i in devices if i - distance in devices]
    return lax.ppermute(block, axis, route)


def extended(array, sides, width):
    for axis, dim in sides:
        size, length = (lax.axis_size(axis), array.shape[dim])
        up = [(i, (i + 1) % size) for i in range(size - 1)]
        down = [(j, i) for i, j in up]
        last = lax.slice_in_dim(array, length - width, length, axis=dim)
        initial = lax.slice_in_dim(array, 0, width, axis=dim)
        before = lax.ppermute(last, axis, up)
        after = lax.ppermute(initial, axis, down)
        array = jnp.concatenate([before, array, after], axis=dim)
    return array


def conv_block(source, weight, frames, rows):
    trimmed = source[:, : frames + 2, :, : rows + 2, :]
    return lax.conv_general_dilated(
        trimmed,
        weight,
        (1, 1, 1),
        ((0, 0), (0, 0), (1, 1)),
        dimension_numbers=("NDCHW", "DHWOI", "NDCHW"),
        preferred_element_type=jnp.float32,
    )


def conv_down(source, weight):
    rows = (source.shape[3] - 1) // 2
    clip_dev = source.shape[0]
    frame_dev = source.shape[1]
    flat = source[:, :, :, : 2 * rows + 1, :].reshape(
        (clip_dev * frame_dev,) + source.shape[2:3] + (2 * rows + 1, source.shape[4])
    )
    total = lax.conv_general_dilated(
        flat,
        weight,
        (2, 2),
        ((0, 0), (1, 1)),
        dimension_numbers=("NCHW", "HWOI", "NCHW"),
        preferred_element_type=jnp.float32,
    )
    return total.reshape((clip_dev, frame_dev) + total.shape[1:])


def finish_rows(first, act_wide, weight_second, live, frame_dev, row_dev):
    second = conv_block(act_wide, weight_second, frame_dev, row_dev) * live
    summed = (first.astype(jnp.float32) + second).astype(jnp.bfloat16)
    above = passed_along(summed[:, :, :, -1:, :], "rows", 1)
    return jnp.concatenate([above, summed], axis=3)


def shards(pixels, frame_counts, weight_first, weight_second, weight_down):
    frame_dev = pixels.shape[1]
    row_dev = pixels.shape[3]
    frame_start = lax.axis_index("frames") * frame_dev
    own_frames = frame_start + jnp.arange(frame_dev, dtype=jnp.int32)
    live = (own_frames[None, :] < frame_counts[:, None]).astype(jnp.float32)[:, :, None, None, None]
    earlier = passed_along(pixels[:, -2:], "frames", 1)
    source = jnp.concatenate([earlier, pixels], axis=1)
    source = extended(source, (("rows", 3),), 1)
    first = (conv_block(source, weight_first, frame_dev, row_dev) * live).astype(jnp.bfloat16)
    act = jax.nn.silu(first.astype(jnp.float32)).astype(jnp.bfloat16)
    act_earlier = passed_along(act[:, -2:], "frames", 1)
    act_wide = jnp.concatenate([act_earlier, act], axis=1)
    act_wide = extended(act_wide, (("rows", 3),), 1)
    summed_pad = finish_rows(first, act_wide, weight_second, live, frame_dev, row_dev)
    return conv_down(summed_pad, weight_down).astype(jnp.bfloat16)


def solution(mesh):
    in_specs = (
        P(("groups", "clips"), "frames", None, "rows", None),
        P(("groups", "clips")),
        P(),
        P(),
        P(),
    )
    out_specs = P(("groups", "clips"), "frames", None, "rows", None)
    return jax.shard_map(shards, mesh=mesh, in_specs=in_specs, out_specs=out_specs, check_vma=False)
```

profile of v0, /device:TPU:0, one launch (start us, length us, event | category | flops | bytes accessed | tf_op | source)
XLA Modules:
  0.0 78.4 jit_solution(1861389486223052510)
XLA Ops:
  0.0 0.0 copy-start
  0.0 0.0 copy-start.4
  0.0 0.0 copy-start.3
  0.0 0.8 slice.21
  0.8 2.4 %collective-permute-start = (bf16[1,2,3,4,256]{4,3,2,1,0:T(4,128)(2,1)S(1)}, bf16[1,2,3,4,256]{4,3,2,1,0:T(4,128)(2,1)S(1)}, u32[]{:S(2)}, u32[]{:S(2)}) collective-permute-start(bf16[1,2,3,4,256]{4,3,2,1,0:T(4,128)(2,1)S(1)} %slice.21), channel_id=1, source_target_pairs={{0,1},{2,3},{4,5},{6,7},{8,9},{10,11},{12,13},{14,15},{16,17},{18,... | collective-permute-start | bytes 36872 | tf_op jit(solution)/shard_map/ppermute | solution.py:10
  3.8 0.2 collective-permute-done
  4.0 0.8 constant_dynamic-update-slice_fusion
  4.8 4.3 %collective-permute-start.1 = (bf16[1,6,3,1,256]{4,3,2,1,0:T(2,128)(2,1)S(1)}, bf16[1,6,3,1,256]{4,3,2,1,0:T(2,128)(2,1)S(1)}, u32[]{:S(2)}, u32[]{:S(2)}) collective-permute-start(bf16[1,6,3,1,256]{4,3,2,1,0:T(2,128)(2,1)S(1)} %get-tuple-element.7), channel_id=1, source_target_pairs={{0,4},{4,8},{8,12},{1,5},{5,9},{9,13},{2,6},{6,10},{10,14},{3,7},{... | collective-permute-start | bytes 27656 | tf_op jit(solution)/shard_map/ppermute | solution.py:20
  9.1 1.3 %collective-permute-start.2 = (bf16[1,6,3,1,256]{4,3,2,1,0:T(2,128)(2,1)S(1)}, bf16[1,6,3,1,256]{4,3,2,1,0:T(2,128)(2,1)S(1)}, u32[]{:S(2)}, u32[]{:S(2)}) collective-permute-start(bf16[1,6,3,1,256]{4,3,2,1,0:T(2,128)(2,1)S(1)} %get-tuple-element.8), channel_id=1, source_target_pairs={{4,0},{8,4},{12,8},{5,1},{9,5},{13,9},{6,2},{10,6},{14,10},{7,3},{... | collective-permute-start | bytes 27656 | tf_op jit(solution)/shard_map/ppermute | solution.py:21
  10.4 0.1 collective-permute-done.1
  10.5 4.2 %collective-permute-done.2 = bf16[1,6,3,1,256]{4,3,2,1,0:T(2,128)(2,1)S(1)} collective-permute-done((bf16[1,6,3,1,256]{4,3,2,1,0:T(2,128)(2,1)S(1)}, bf16[1,6,3,1,256]{4,3,2,1,0:T(2,128)(2,1)S(1)}, u32[]{:S(2)}, u32[]{:S(2)}) %collective-permute-start.2) | collective-permute-done | bytes 9248 | tf_op jit(solution)/shard_map/ppermute | solution.py:21
  14.7 0.1 maximum_bitcast_fusion.2
  14.8 0.1 pad
  14.9 0.2 reshape.22
  15.1 1.1 %copy.40 = bf16[6,3,6,1,8,33]{4,1,5,2,0,3:T(4,128)(2,1)S(1)} copy(bf16[6,3,6,1,8,33]{5,4,2,1,0,3:T(8,128)(2,1)S(1)} %reshape.22) | data formatting | bytes 114048 | tf_op jit(solution)/shard_map/conv_general_dilated | solution.py:28
  16.3 0.1 slice.40
  16.4 0.0 copy-done.4
  16.4 0.0 copy-done.3
  16.4 5.8 %fusion.13 = (bf16[4,4,8,33,64]{4,2,3,1,0:T(8,128)(2,1)S(1)}, bf16[4,4,8,33,64]{4,2,3,1,0:T(8,128)(2,1)}) fusion(f32[4]{0:T(128)S(1)} %compare_convert_fusion, bf16[3,3,3,64,3]{3,4,2,1,0:T(4,128)(2,1)S(1)} %copy-done.3, bf16[6,3,6,1,7,2]{4,1,5,2,0,3:T(4,128)(2,1)S(1)} %slice.40, bf16[6,3,6,1,8,33]{4,1,5,2,0,3:T(4,128)(2,1)S(1)} %copy.40, ...), kind=kOutput, calls=%fused_computation.18 | convolution fusion | flops 46408896 | bytes 1152040 | tf_op jit(solution)/shard_map/conv_general_dilated | solution.py:28
  22.3 0.4 copy.42
  22.7 0.2 copy.41
  22.9 0.2 slice_bitcast_fusion.2
  23.1 1.3 %collective-permute-start.3 = (bf16[1,2,64,4,256]{2,3,4,1,0:T(4,128)(2,1)S(1)}, bf16[1,2,64,4,256]{2,3,4,1,0:T(4,128)(2,1)S(1)}, u32[]{:S(2)}, u32[]{:S(2)}) collective-permute-start(bf16[1,2,64,4,256]{2,3,4,1,0:T(4,128)(2,1)S(1)} %slice_bitcast_fusion.2), channel_id=1, source_target_pairs={{0,1},{2,3},{4,5},{6,7},{8,9},{10,11},{12,13},{14,15},{16,17},{18,... | collective-permute-start | bytes 786440 | tf_op jit(solution)/shard_map/ppermute | solution.py:10
  24.4 0.4 slice_bitcast_fusion.1
  24.8 1.1 %collective-permute-done.3 = bf16[1,2,64,4,256]{2,3,4,1,0:T(4,128)(2,1)S(1)} collective-permute-done((bf16[1,2,64,4,256]{2,3,4,1,0:T(4,128)(2,1)S(1)}, bf16[1,2,64,4,256]{2,3,4,1,0:T(4,128)(2,1)S(1)}, u32[]{:S(2)}, u32[]{:S(2)}) %collective-permute-start.3) | collective-permute-done | bytes 262176 | tf_op jit(solution)/shard_map/ppermute | solution.py:10
  25.9 0.0 copy-start.1
  25.9 2.3 %fusion.34 = (bf16[1,6,64,1,256]{2,3,4,1,0:T(2,128)(2,1)S(1)}, bf16[1,6,64,1,256]{2,3,4,1,0:T(2,128)(2,1)S(1)}) fusion(bf16[1,4,64,4,256]{2,3,4,1,0:T(4,128)(2,1)S(1)} %slice_bitcast_fusion.1, bf16[1,2,64,4,256]{2,3,4,1,0:T(4,128)(2,1)S(1)} %collective-permute-done.3), kind=kLoop, calls=%fused_computation.41 | loop fusion | flops 196608 | bytes 1179648 | tf_op jit(solution)/shard_map/concatenate | solution.py:75
  28.2 0.0 copy-done.1
  28.2 1.5 %copy.43 = bf16[1,6,64,1,256]{4,2,3,1,0:T(8,128)(2,1)} copy(bf16[1,6,64,1,256]{2,3,4,1,0:T(2,128)(2,1)S(1)} %get-tuple-element.5) | data formatting | bytes 393216 | tf_op jit(solution)/shard_map/slice | solution.py:18
  29.7 1.5 %copy.44 = bf16[1,6,64,1,256]{4,2,3,1,0:T(8,128)(2,1)} copy(bf16[1,6,64,1,256]{2,3,4,1,0:T(2,128)(2,1)S(1)} %get-tuple-element.6) | data formatting | bytes 393216 | tf_op jit(solution)/shard_map/slice | solution.py:19
  31.3 1.3 %collective-permute-start.5 = (bf16[1,6,64,1,256]{4,2,3,1,0:T(8,128)(2,1)}, bf16[1,6,64,1,256]{4,2,3,1,0:T(8,128)(2,1)S(1)}, u32[]{:S(2)}, u32[]{:S(2)}) collective-permute-start(bf16[1,6,64,1,256]{4,2,3,1,0:T(8,128)(2,1)} %copy.44), channel_id=1, source_target_pairs={{4,0},{8,4},{12,8},{5,1},{9,5},{13,9},{6,2},{10,6},{14,10},{7,3},{... | collective-permute-start | bytes 589832 | tf_op jit(solution)/shard_map/ppermute | solution.py:21
  32.5 4.7 %collective-permute-start.4 = (bf16[1,6,64,1,256]{4,2,3,1,0:T(8,128)(2,1)}, bf16[1,6,64,1,256]{4,2,3,1,0:T(8,128)(2,1)S(1)}, u32[]{:S(2)}, u32[]{:S(2)}) collective-permute-start(bf16[1,6,64,1,256]{4,2,3,1,0:T(8,128)(2,1)} %copy.43), channel_id=1, source_target_pairs={{0,4},{4,8},{8,12},{1,5},{5,9},{9,13},{2,6},{6,10},{10,14},{3,7},{... | collective-permute-start | bytes 589832 | tf_op jit(solution)/shard_map/ppermute | solution.py:20
  37.3 2.3 %pad_maximum_fusion = bf16[1,6,64,4,256]{2,3,4,1,0:T(4,128)(2,1)S(1)} fusion(bf16[1,2,64,4,256]{2,3,4,1,0:T(4,128)(2,1)} %copy-done.1, bf16[1,4,64,4,256]{2,3,4,1,0:T(4,128)(2,1)S(1)} %slice_bitcast_fusion.1), kind=kLoop, calls=%fused_computation.23 | loop fusion | flops 393216 | bytes 1572864 | tf_op jit(solution)/shard_map/concatenate | solution.py:75
  39.5 0.8 %copy.45 = bf16[1,6,64,4,256]{4,2,3,1,0:T(8,128)(2,1)S(1)} copy(bf16[1,6,64,4,256]{2,3,4,1,0:T(4,128)(2,1)S(1)} %pad_maximum_fusion) | data formatting | bytes 1572864 | tf_op jit(solution)/shard_map/concatenate | solution.py:75
  40.3 0.2 collective-permute-done.5
  40.5 1.3 %collective-permute-done.4 = bf16[1,6,64,1,256]{4,2,3,1,0:T(8,128)(2,1)S(1)} collective-permute-done((bf16[1,6,64,1,256]{4,2,3,1,0:T(8,128)(2,1)}, bf16[1,6,64,1,256]{4,2,3,1,0:T(8,128)(2,1)S(1)}, u32[]{:S(2)}, u32[]{:S(2)}) %collective-permute-start.4) | collective-permute-done | bytes 196640 | tf_op jit(solution)/shard_map/ppermute | solution.py:20
  41.8 0.1 maximum_bitcast_fusion
  42.0 0.7 pad.2
  42.7 5.4 %reshape.58 = bf16[6,64,6,1,8,33]{5,4,1,2,0,3:T(8,128)(2,1)} reshape(bf16[6,64,6,1,264]{4,1,2,0,3:T(8,128)(2,1)S(1)} %pad.2) | data formatting | bytes 2433024 | tf_op jit(solution)/shard_map/conv_general_dilated | solution.py:28
  48.1 6.0 %copy.48 = bf16[6,64,6,1,8,33]{1,4,5,2,0,3:T(8,128)(2,1)S(1)} copy(bf16[6,64,6,1,8,33]{5,4,1,2,0,3:T(8,128)(2,1)} %reshape.58) | data formatting | bytes 2433024 | tf_op jit(solution)/shard_map/conv_general_dilated | solution.py:28
  54.1 0.0 copy-done
  54.1 9.0 %fusion.14 = bf16[4,4,8,33,64]{4,2,3,1,0:T(8,128)(2,1)S(1)} fusion(bf16[4,4,8,33,64]{4,2,3,1,0:T(8,128)(2,1)} %get-tuple-element.10, bf16[3,3,3,64,64]{4,3,2,1,0:T(8,128)(2,1)S(1)} %copy-done, bf16[6,64,6,1,7,2]{1,4,5,2,0,3:T(8,128)(2,1)S(1)} %slice.48, bf16[6,64,6,1,8,33]{1,4,5,2,0,3:T(8,128)(2,1)S(1)} %copy.48, f32[4]{0:T(128)S(1)} %compare_convert_fusion, ...), kind=kOutput, calls=%fused_computation.19 | convolution fusion | flops 939503616 | bytes 2583832 | tf_op jit(solution)/shard_map/conv_general_dilated | solution.py:28
  63.1 0.4 copy.50
  63.5 0.1 copy.49
  63.6 0.1 slice_bitcast_fusion.4
  63.7 4.5 %collective-permute-start.6 = (bf16[1,4,64,1,256]{2,1,4,0,3:T(4,128)(2,1)S(1)}, bf16[1,4,64,1,256]{2,1,4,0,3:T(4,128)(2,1)S(1)}, u32[]{:S(2)}, u32[]{:S(2)}) collective-permute-start(bf16[1,4,64,1,256]{2,1,4,0,3:T(4,128)(2,1)S(1)} %slice_bitcast_fusion.4), channel_id=1, source_target_pairs={{0,4},{4,8},{8,12},{1,5},{5,9},{9,13},{2,6},{6,10},{10,14},{3,7},{... | collective-permute-start | bytes 393224 | tf_op jit(solution)/shard_map/ppermute | solution.py:10
  68.3 0.4 slice_bitcast_fusion
  68.6 0.5 copy.52
  69.2 3.8 %collective-permute-done.6 = bf16[1,4,64,1,256]{2,1,4,0,3:T(4,128)(2,1)S(1)} collective-permute-done((bf16[1,4,64,1,256]{2,1,4,0,3:T(4,128)(2,1)S(1)}, bf16[1,4,64,1,256]{2,1,4,0,3:T(4,128)(2,1)S(1)}, u32[]{:S(2)}, u32[]{:S(2)}) %collective-permute-start.6) | collective-permute-done | bytes 131104 | tf_op jit(solution)/shard_map/ppermute | solution.py:10
  73.0 0.2 copy.51
  73.1 0.1 maximum_bitcast_fusion.1
  73.2 1.5 %copy.59 = bf16[64,5,4,256]{0,2,3,1:T(4,128)(2,1)S(1)} copy(bf16[64,5,4,256]{3,0,1,2:T(8,128)(2,1)S(1)} %maximum_bitcast_fusion.1) | data formatting | bytes 1310720
  74.7 0.7 pad.4.clone
  75.4 0.0 copy-start.2
  75.4 0.0 copy-start.5
  75.5 0.8 %fusion.17 = bf16[64,5,4,8,36]{0,2,4,3,1:T(4,128)(2,1)S(1)} fusion(bf16[64,5,4,7,2]{0,2,4,3,1:T(4,128)(2,1)S(1)} %slice.52, bf16[64,5,4,8,34]{0,2,4,3,1:T(4,128)(2,1)S(1)} %bitcast.55), kind=kLoop, calls=%fused_computation.24 | loop fusion | flops 2211840 | bytes 1469440 | tf_op jit(solution)/shard_map/conv_general_dilated | solution.py:45
  76.3 0.1 copy-done.2
  76.3 0.0 copy-done.5
  76.3 0.8 %fusion.31 = bf16[2,32,17,64]{3,1,2,0:T(8,128)(2,1)S(1)} fusion(bf16[3,3,64,64]{3,2,1,0:T(8,128)(2,1)S(1)} %copy-done.2, bf16[64,5,4,8,36]{0,2,4,3,1:T(4,128)(2,1)S(1)} %fusion.17, pred[32,17]{0,1:T(8,128)(4,1)S(1)} %copy-done.5), kind=kOutput, calls=%fused_computation.37 | convolution fusion | flops 80355328 | bytes 950816 | tf_op jit(solution)/shard_map/conv_general_dilated | solution.py:45
  77.1 0.2 copy.55
  77.4 0.2 slice_bitcast_fusion.3
  77.6 0.8 %copy.56 = bf16[1,4,64,2,128]{4,3,2,1,0:T(2,128)(2,1)} copy(bf16[1,4,64,2,128]{2,3,4,1,0:T(2,128)(2,1)S(1)} %slice_bitcast_fusion.3) | data formatting | bytes 262144 | tf_op jit(solution)/shard_map/convert_element_type | solution.py:78
  (7 shorter events, 0.2 us)
Async XLA Ops:
  0.0 54.1 %copy-start = (bf16[3,3,3,64,64]{4,3,2,1,0:T(8,128)(2,1)S(1)}, bf16[3,3,3,64,64]{4,3,2,1,0:T(8,128)(2,1)}, u32[]{:S(2)}) copy-start(bf16[3,3,3,64,64]{4,3,2,1,0:T(8,128)(2,1)} %param.8) | copy-start | bytes 663556
  0.0 16.4 %copy-start.4 = (pred[8,33]{0,1:T(8,128)(4,1)S(1)}, pred[8,33]{0,1:T(8,128)(4,1)}, u32[]{:S(2)}) copy-start(pred[8,33]{0,1:T(8,128)(4,1)} %constant.24) | copy-start | bytes 796
  0.0 16.4 %copy-start.3 = (bf16[3,3,3,64,3]{3,4,2,1,0:T(4,128)(2,1)S(1)}, bf16[3,3,3,64,3]{3,4,2,1,0:T(4,128)(2,1)}, u32[]{:S(2)}) copy-start(bf16[3,3,3,64,3]{3,4,2,1,0:T(4,128)(2,1)} %param.7) | copy-start | bytes 31108
  0.8 3.2 %collective-permute-start = (bf16[1,2,3,4,256]{4,3,2,1,0:T(4,128)(2,1)S(1)}, bf16[1,2,3,4,256]{4,3,2,1,0:T(4,128)(2,1)S(1)}, u32[]{:S(2)}, u32[]{:S(2)}) collective-permute-start(bf16[1,2,3,4,256]{4,3,2,1,0:T(4,128)(2,1)S(1)} %slice.21), channel_id=1, source_target_pairs={{0,1},{2,3},{4,5},{6,7},{8,9},{10,11},{12,13},{14,15},{16,17},{18,... | collective-permute-start | bytes 36872 | tf_op jit(solution)/shard_map/ppermute | solution.py:10
  4.8 5.8 %collective-permute-start.1 = (bf16[1,6,3,1,256]{4,3,2,1,0:T(2,128)(2,1)S(1)}, bf16[1,6,3,1,256]{4,3,2,1,0:T(2,128)(2,1)S(1)}, u32[]{:S(2)}, u32[]{:S(2)}) collective-permute-start(bf16[1,6,3,1,256]{4,3,2,1,0:T(2,128)(2,1)S(1)} %get-tuple-element.7), channel_id=1, source_target_pairs={{0,4},{4,8},{8,12},{1,5},{5,9},{9,13},{2,6},{6,10},{10,14},{3,7},{... | collective-permute-start | bytes 27656 | tf_op jit(solution)/shard_map/ppermute | solution.py:20
  9.1 5.7 %collective-permute-start.2 = (bf16[1,6,3,1,256]{4,3,2,1,0:T(2,128)(2,1)S(1)}, bf16[1,6,3,1,256]{4,3,2,1,0:T(2,128)(2,1)S(1)}, u32[]{:S(2)}, u32[]{:S(2)}) collective-permute-start(bf16[1,6,3,1,256]{4,3,2,1,0:T(2,128)(2,1)S(1)} %get-tuple-element.8), channel_id=1, source_target_pairs={{4,0},{8,4},{12,8},{5,1},{9,5},{13,9},{6,2},{10,6},{14,10},{7,3},{... | collective-permute-start | bytes 27656 | tf_op jit(solution)/shard_map/ppermute | solution.py:21
  23.1 2.8 %collective-permute-start.3 = (bf16[1,2,64,4,256]{2,3,4,1,0:T(4,128)(2,1)S(1)}, bf16[1,2,64,4,256]{2,3,4,1,0:T(4,128)(2,1)S(1)}, u32[]{:S(2)}, u32[]{:S(2)}) collective-permute-start(bf16[1,2,64,4,256]{2,3,4,1,0:T(4,128)(2,1)S(1)} %slice_bitcast_fusion.2), channel_id=1, source_target_pairs={{0,1},{2,3},{4,5},{6,7},{8,9},{10,11},{12,13},{14,15},{16,17},{18,... | collective-permute-start | bytes 786440 | tf_op jit(solution)/shard_map/ppermute | solution.py:10
  25.9 2.3 %copy-start.1 = (bf16[1,2,64,4,256]{2,3,4,1,0:T(4,128)(2,1)}, bf16[1,2,64,4,256]{2,3,4,1,0:T(4,128)(2,1)S(1)}, u32[]{:S(2)}) copy-start(bf16[1,2,64,4,256]{2,3,4,1,0:T(4,128)(2,1)S(1)} %collective-permute-done.3) | copy-start | bytes 786436
  31.3 9.3 %collective-permute-start.5 = (bf16[1,6,64,1,256]{4,2,3,1,0:T(8,128)(2,1)}, bf16[1,6,64,1,256]{4,2,3,1,0:T(8,128)(2,1)S(1)}, u32[]{:S(2)}, u32[]{:S(2)}) collective-permute-start(bf16[1,6,64,1,256]{4,2,3,1,0:T(8,128)(2,1)} %copy.44), channel_id=1, source_target_pairs={{4,0},{8,4},{12,8},{5,1},{9,5},{13,9},{6,2},{10,6},{14,10},{7,3},{... | collective-permute-start | bytes 589832 | tf_op jit(solution)/shard_map/ppermute | solution.py:21
  32.5 9.3 %collective-permute-start.4 = (bf16[1,6,64,1,256]{4,2,3,1,0:T(8,128)(2,1)}, bf16[1,6,64,1,256]{4,2,3,1,0:T(8,128)(2,1)S(1)}, u32[]{:S(2)}, u32[]{:S(2)}) collective-permute-start(bf16[1,6,64,1,256]{4,2,3,1,0:T(8,128)(2,1)} %copy.43), channel_id=1, source_target_pairs={{0,4},{4,8},{8,12},{1,5},{5,9},{9,13},{2,6},{6,10},{10,14},{3,7},{... | collective-permute-start | bytes 589832 | tf_op jit(solution)/shard_map/ppermute | solution.py:20
  63.7 9.2 %collective-permute-start.6 = (bf16[1,4,64,1,256]{2,1,4,0,3:T(4,128)(2,1)S(1)}, bf16[1,4,64,1,256]{2,1,4,0,3:T(4,128)(2,1)S(1)}, u32[]{:S(2)}, u32[]{:S(2)}) collective-permute-start(bf16[1,4,64,1,256]{2,1,4,0,3:T(4,128)(2,1)S(1)} %slice_bitcast_fusion.4), channel_id=1, source_target_pairs={{0,4},{4,8},{8,12},{1,5},{5,9},{9,13},{2,6},{6,10},{10,14},{3,7},{... | collective-permute-start | bytes 393224 | tf_op jit(solution)/shard_map/ppermute | solution.py:10
  75.4 0.9 %copy-start.2 = (bf16[3,3,64,64]{3,2,1,0:T(8,128)(2,1)S(1)}, bf16[3,3,64,64]{3,2,1,0:T(8,128)(2,1)}, u32[]{:S(2)}) copy-start(bf16[3,3,64,64]{3,2,1,0:T(8,128)(2,1)} %param.9) | copy-start | bytes 221188
  75.4 0.9 %copy-start.5 = (pred[32,17]{0,1:T(8,128)(4,1)S(1)}, pred[32,17]{0,1:T(8,128)(4,1)}, u32[]{:S(2)}) copy-start(pred[32,17]{0,1:T(8,128)(4,1)} %constant.23) | copy-start | bytes 1636
where the time goes:
time: 78.9 us; the launch traced here: 78.4 us
  local copies, waits for them, and re-layouts  25.4 us (32%)
  starting transfers between devices  19.8 us (25%)
  matrix products  15.6 us (20%)
  waiting for transfers between devices  10.9 us (14%)
  other arithmetic  5.58 us (7%)
  between operations  1.01 us (1%)
    conv_general_dilated x2, matrix products, conv_block(): lax.conv_general_dilated(trimmed, weight, (1, 1, 1), ((0, 0), (0, 0), (1,...  14.8 us
    conv_general_dilated x6, local copies, waits for them, and re-layouts, conv_block(): lax.conv_general_dilated(trimmed, weight, (1, 1, 1), ((0, 0), (0, 0), (1,...  12.8 us
    ppermute x2, starting transfers between devices, extended(): before = lax.ppermute(last, axis, up)  9.04 us
    ppermute x3, starting transfers between devices, passed_along(): return lax.ppermute(block, axis, route)  8.23 us
    ppermute x3, waiting for transfers between devices, passed_along(): return lax.ppermute(block, axis, route)  5.08 us
    concatenate x2, other arithmetic, shards(): act_wide = jnp.concatenate([act_earlier, act], axis=1)  4.52 us
    ppermute x2, waiting for transfers between devices, extended(): after = lax.ppermute(initial, axis, down)  4.39 us
    ppermute x2, starting transfers between devices, extended(): after = lax.ppermute(initial, axis, down)  2.57 us
  transfers between devices with their start and end apart: 7, of which 7 were waited for; matrix products, arithmetic and copies ran while one was open for 5% of the time, Pallas kernels for 0%

commit v1 on v0

v1 whole, which is shorter than its diff:
```python
import jax
import jax.numpy as jnp
import numpy as np
from jax import lax
from jax.experimental import pallas as pl
from jax.experimental.pallas import tpu as pltpu
from jax.sharding import PartitionSpec as P

VIEWS = 4
PARITIES = 2
TAPS = 3
SLOT = 16

VMEM = pl.BlockSpec(memory_space=pltpu.VMEM)
SMEM = pl.BlockSpec(memory_space=pltpu.SMEM)


def view_columns(width):
    half = width // 2
    select = np.zeros((width, VIEWS * half), np.float32)
    for view in range(VIEWS):
        for x in range(half):
            column = 2 * x + view - 1
            if 0 <= column < width:
                select[column, view * half + x] = 1
    return select


def first_places(rows, colors):
    sources = 3
    places = np.zeros((rows + 3, PARITIES, TAPS, TAPS, TAPS, colors, TAPS, VIEWS, sources, SLOT), np.float32)
    for row in range(rows + 3):
        for tap_y in range(TAPS):
            pixel_row = row + tap_y - 3
            if pixel_row < 0:
                source, local = 1, pixel_row + rows
            elif pixel_row < rows:
                source, local = 0, pixel_row
            else:
                source, local = 2, pixel_row - rows
            for parity in range(PARITIES):
                for tap_t in range(TAPS):
                    for tap_x in range(TAPS):
                        for color in range(colors):
                            places[row, parity, tap_t, tap_y, tap_x, color, tap_t, tap_x + parity, source, color * rows + local] = 1
    return places.reshape((rows + 3) * PARITIES, TAPS**3 * colors, TAPS * VIEWS * sources * SLOT)


def prepare_kernel(first_ref, places_ref, second_ref, down_ref, first_out, second_out, down_out):
    channels = first_ref.shape[0]
    first = first_ref[...]
    for block in range(places_ref.shape[0]):
        placed = jnp.dot(first, places_ref[block], preferred_element_type=jnp.float32)
        first_out[block * channels:(block + 1) * channels, :] = placed.astype(jnp.bfloat16)
    none = jnp.zeros((channels, channels), jnp.bfloat16)
    for tap_t in range(TAPS):
        for tap_y in range(TAPS):
            base = (tap_t * TAPS + tap_y) * TAPS
            taps = [second_ref[base + tap_x] for tap_x in range(TAPS)]
            columns = slice(base // TAPS * VIEWS * channels, (base // TAPS + 1) * VIEWS * channels)
            second_out[:channels, columns] = jnp.concatenate(taps + [none], axis=1)
            second_out[channels:, columns] = jnp.concatenate([none] + taps, axis=1)
    out_rows = down_out.shape[0] // channels
    sum_rows = down_out.shape[1] // (TAPS * channels)
    taps = jnp.concatenate([down_ref[tap] for tap in range(TAPS * TAPS)], axis=1)
    place = lax.broadcasted_iota(jnp.int32, (down_out.shape[0], channels), 0)
    channel = lax.broadcasted_iota(jnp.int32, (down_out.shape[0], channels), 1)
    total = None
    for y in range(out_rows):
        spread = (place == channel * out_rows + y).astype(jnp.float32).astype(jnp.bfloat16)
        pieces = [taps]
        before, after = 2 * y, sum_rows - TAPS - 2 * y
        if before:
            pieces = [jnp.zeros((channels, before * TAPS * channels), jnp.bfloat16)] + pieces
        if after:
            pieces = pieces + [jnp.zeros((channels, after * TAPS * channels), jnp.bfloat16)]
        part = jnp.dot(spread, jnp.concatenate(pieces, axis=1), preferred_element_type=jnp.float32)
        total = part if total is None else total + part
    down_out[...] = total.astype(jnp.bfloat16)


def encode_kernel(count_ref, own_ref, above_ref, below_ref, columns_ref, first_w, second_w, down_w, out_ref, views, act, held, taps, *, rows, frames):
    half = columns_ref.shape[1] // VIEWS
    channels = second_w.shape[0] // PARITIES
    pair = PARITIES * channels
    wide = (frames + 2) * half
    narrow = frames * half
    for source, ref in enumerate((own_ref, above_ref, below_ref)):
        spread = jnp.dot(ref[...], columns_ref[...], preferred_element_type=jnp.float32).astype(jnp.bfloat16)
        for view in range(VIEWS):
            place = (view * 3 + source) * SLOT
            for t in range(frames + 4):
                views[place:place + SLOT, t * half:(t + 1) * half] = spread[t * SLOT:(t + 1) * SLOT, view * half:(view + 1) * half]

    start = lax.axis_index("frames") * frames
    row_start = lax.axis_index("rows") * rows
    height = lax.axis_size("rows") * rows
    slot = lax.broadcasted_iota(jnp.int32, (1, wide), 1)
    live = (slot // half + (start - 2) < count_ref[0]).astype(jnp.float32)
    lane = lax.broadcasted_iota(jnp.int32, (channels, half), 1)
    depth = views.shape[0]
    for row in range(rows + 3):
        inside = jnp.logical_and(row_start + (row - 2) >= 0, row_start + (row - 2) < height).astype(jnp.float32)
        total = None
        for tap in range(TAPS):
            part = jnp.dot(
                first_w[row * pair:(row + 1) * pair, tap * depth:(tap + 1) * depth],
                views[:, tap * half:tap * half + wide],
                preferred_element_type=jnp.float32,
            )
            total = part if total is None else total + part
        first = (total * (live * inside)).astype(jnp.bfloat16)
        if 1 <= row <= rows + 1:
            held[(row - 1) * pair:row * pair, :] = first[:, 2 * half:]
        value = first.astype(jnp.float32)
        value = value / (1 + jnp.exp(-value))
        base = row * VIEWS * channels
        act[base + channels:base + 3 * channels, :] = value.astype(jnp.bfloat16)
        for t in range(frames + 2):
            lanes = slice(t * half, (t + 1) * half)
            left = jnp.where(lane == 0, 0.0, pltpu.roll(value[channels:, lanes], 1, 1))
            right = jnp.where(lane == half - 1, 0.0, pltpu.roll(value[:channels, lanes], half - 1, 1))
            act[base:base + channels, lanes] = left.astype(jnp.bfloat16)
            act[base + 3 * channels:base + 4 * channels, lanes] = right.astype(jnp.bfloat16)

    window = TAPS * VIEWS * channels
    for row in range(rows + 1):
        base = row * VIEWS * channels
        total = None
        for tap in range(TAPS):
            part = jnp.dot(
                second_w[:, tap * window:(tap + 1) * window],
                act[base:base + window, tap * half:tap * half + narrow],
                preferred_element_type=jnp.float32,
            )
            total = part if total is None else total + part
        inside = (row_start + (row - 1) >= 0).astype(jnp.float32)
        second = total * (live[:, 2 * half:] * inside)
        value = (held[row * pair:(row + 1) * pair, :].astype(jnp.float32) + second).astype(jnp.bfloat16)
        base = row * TAPS * channels
        taps[base + channels:base + 3 * channels, :] = value
        value = value.astype(jnp.float32)
        for t in range(frames):
            lanes = slice(t * half, (t + 1) * half)
            left = jnp.where(lane == 0, 0.0, pltpu.roll(value[channels:, lanes], 1, 1))
            taps[base:base + channels, lanes] = left.astype(jnp.bfloat16)
    encoded = jnp.dot(down_w[...], taps[...], preferred_element_type=jnp.float32).astype(jnp.bfloat16)
    size = down_w.shape[0]
    for t in range(frames):
        out_ref[t * size:(t + 1) * size, :] = encoded[:, t * half:(t + 1) * half]


def packed(pixels):
    frames, colors, rows, width = pixels.shape
    flat = pixels.reshape(frames, colors * rows, width)
    return jnp.pad(flat, ((0, 0), (0, SLOT - colors * rows), (0, 0))).reshape(frames * SLOT, width)


def shards(pixels, frame_counts, weight_first, weight_second, weight_down):
    clips, frames, colors, rows, width = pixels.shape
    channels = weight_first.shape[3]
    half = width // 2
    out_rows = rows // 2
    frame_devices, row_devices = lax.axis_size("frames"), lax.axis_size("rows")
    assert clips == 1 and frames >= 4 and rows >= 3 and rows % 2 == 0 and colors * rows <= SLOT
    earlier = lax.ppermute(pixels[:, -4:], "frames", [(i, i + 1) for i in range(frame_devices - 1)])
    own = jnp.concatenate([packed(earlier[0]), packed(pixels[0])], axis=0)
    above = lax.ppermute(own, "rows", [(i, i + 1) for i in range(row_devices - 1)])
    below = lax.ppermute(own, "rows", [(i + 1, i) for i in range(row_devices - 1)])

    bf16 = jnp.bfloat16
    places = jnp.asarray(first_places(rows, colors), bf16)
    columns = jnp.asarray(view_columns(width), bf16)
    pair = PARITIES * channels
    first_w, second_w, down_w = pl.pallas_call(
        prepare_kernel,
        name="prepare",
        compiler_params=pltpu.CompilerParams(vmem_limit_bytes=8 << 20),
        in_specs=[VMEM] * 4,
        out_specs=[VMEM] * 3,
        out_shape=[
            jax.ShapeDtypeStruct(((rows + 3) * pair, places.shape[2]), bf16),
            jax.ShapeDtypeStruct((pair, TAPS * TAPS * VIEWS * channels), bf16),
            jax.ShapeDtypeStruct((channels * out_rows, (rows + 1) * TAPS * channels), bf16),
        ],
    )(
        weight_first.transpose(3, 0, 1, 2, 4).reshape(channels, TAPS**3 * colors),
        places,
        weight_second.reshape(TAPS**3, channels, channels),
        weight_down.reshape(TAPS**2, channels, channels),
    )
    wide, narrow = (frames + 2) * half, frames * half
    encoded = pl.pallas_call(
        lambda *refs: encode_kernel(*refs, rows=rows, frames=frames),
        name="encode",
        compiler_params=pltpu.CompilerParams(vmem_limit_bytes=24 << 20),
        in_specs=[SMEM] + [VMEM] * 7,
        out_specs=VMEM,
        out_shape=jax.ShapeDtypeStruct((frames * channels * out_rows, half), bf16),
        scratch_shapes=[
            pltpu.VMEM((VIEWS * 3 * SLOT, (frames + 4) * half), bf16),
            pltpu.VMEM(((rows + 3) * VIEWS * channels, wide), bf16),
            pltpu.VMEM(((rows + 1) * pair, narrow), bf16),
            pltpu.VMEM(((rows + 1) * TAPS * channels, narrow), bf16),
        ],
    )(frame_counts, own, above, below, columns, first_w, second_w, down_w)
    return encoded.reshape(1, frames, channels, out_rows, half)


def solution(mesh):
    in_specs = (
        P(("groups", "clips"), "frames", None, "rows", None),
        P(("groups", "clips")),
        P(),
        P(),
        P(),
    )
    out_specs = P(("groups", "clips"), "frames", None, "rows", None)
    return jax.shard_map(shards, mesh=mesh, in_specs=in_specs, out_specs=out_specs, check_vma=False)
```

time: 78.9 us -> 20.1 us (0.25)
  local copies, waits for them, and re-layouts: 25.4 us -> 5 us
  matrix products: 15.6 us -> 0 us
  starting transfers between devices: 19.8 us -> 8.74 us
  waiting for transfers between devices: 10.9 us -> 0.26 us
  other arithmetic: 5.58 us -> 0.01 us
  Pallas kernels: 0 us -> 4.99 us
    conv_general_dilated x3 -> x0, matrix products: 15.6 us -> none  [the longest x2 14.8 us: conv_block(): lax.conv_general_dilated(trimmed, weight, (1, 1, 1), ((0, 0), (0, 0), (1,...]
    conv_general_dilated x7 -> x0, local copies, waits for them, and re-layouts: 12.8 us -> none  [the longest x6 12.8 us: conv_block(): lax.conv_general_dilated(trimmed, weight, (1, 1, 1), ((0, 0), (0, 0), (1,...]
    ppermute x7 -> x3, starting transfers between devices: 19.8 us -> 8.74 us  [the longest x1 4.93 us: shards(): lax.ppermute(own, 'rows', [(i, i + 1) for i in range(row_devices - 1)])]
    ppermute x7 -> x3, waiting for transfers between devices: 10.9 us -> 0.26 us  [the longest x1 0.26 us: shards(): lax.ppermute(pixels[:, -4:], 'frames', [(i, i + 1) for i in range(frame_d...]
    pallas_call x0 -> x2, Pallas kernels: none -> 4.99 us  [the longest x1 4.41 us: shards(): pl.pallas_call(lambda *refs: encode_kernel(*refs, rows=rows, frames=frame...]
    concatenate x4 -> x1, other arithmetic: 4.73 us -> 0.01 us  [shards(): own = jnp.concatenate([packed(earlier[0]), packed(pixels[0])], axis=0)]
    slice x6 -> x0, local copies, waits for them, and re-layouts: 4.13 us -> none  [the longest x2 1.56 us: extended(): last = lax.slice_in_dim(array, length - width, length, axis=dim)]
    convert_element_type x12 -> x0, local copies, waits for them, and re-layouts: 3.67 us -> none  [the longest x5 1.44 us: finish_rows(): summed = (first.astype(jnp.float32) + second).astype(jnp.bfloat16)]
  transfers between devices with their start and end apart: 7 -> 3, of which waited for: 7 -> 1; matrix products, arithmetic and copies ran while one was open for 5% -> 8% of each run, Pallas kernels for 0% -> 3%
where the time goes in v1:
time: 20.1 us; the launch traced here: 19.8 us
  starting transfers between devices  8.74 us (43%)
  local copies, waits for them, and re-layouts  5 us (25%)
  Pallas kernels  4.99 us (25%)
  between operations  0.76 us (4%)
  waiting for transfers between devices  0.26 us (1%)
    ppermute x1, starting transfers between devices, shards(): lax.ppermute(own, 'rows', [(i, i + 1) for i in range(row_devices - 1)])  4.93 us
    pallas_call x1, Pallas kernels, shards(): pl.pallas_call(lambda *refs: encode_kernel(*refs, rows=rows, frames=frame...  4.41 us
    unnamed x11, local copies, waits for them, and re-layouts  4.1 us
    ppermute x1, starting transfers between devices, shards(): lax.ppermute(pixels[:, -4:], 'frames', [(i, i + 1) for i in range(frame_d...  2.52 us
    ppermute x1, starting transfers between devices, shards(): lax.ppermute(own, 'rows', [(i + 1, i) for i in range(row_devices - 1)])  1.29 us
    reshape x2, local copies, waits for them, and re-layouts, shards(): weight_first.transpose(3, 0, 1, 2, 4).reshape(channels, TAPS ** 3 * colors)  0.87 us
    pallas_call x1, Pallas kernels, shards(): pl.pallas_call(prepare_kernel, name='prepare', compiler_params=pltpu.Comp...  0.58 us
  transfers between devices with their start and end apart: 3, of which 1 were waited for; matrix products, arithmetic and copies ran while one was open for 8% of the time, Pallas kernels for 3%

profile of v1, /device:TPU:0, one launch (start us, length us, event | category | flops | bytes accessed | tf_op | source)
XLA Modules:
  0.0 19.8 jit_solution(7040132872077441564)
XLA Ops:
  0.0 0.0 copy-start.2
  0.0 2.5 %collective-permute-start = (bf16[1,4,3,4,256]{4,3,2,1,0:T(4,128)(2,1)}, bf16[1,4,3,4,256]{4,3,2,1,0:T(4,128)(2,1)S(1)}, u32[]{:S(2)}, u32[]{:S(2)}) collective-permute-start(bf16[1,4,3,4,256]{4,3,2,1,0:T(4,128)(2,1)} %param.7), channel_id=1, source_target_pairs={{0,1},{2,3},{4,5},{6,7},{8,9},{10,11},{12,13},{14,15},{16,17},{18,... | collective-permute-start | bytes 73736 | tf_op jit(solution)/shard_map/ppermute | solution.py:166
  2.5 0.7 %copy.11 = bf16[1,4,3,4,256]{4,1,3,2,0:T(4,128)(2,1)S(1)} copy(bf16[1,4,3,4,256]{4,3,2,1,0:T(4,128)(2,1)} %param.7) | data formatting | bytes 49152 | tf_op args[0]
  3.3 0.3 %collective-permute-done = bf16[1,4,3,4,256]{4,3,2,1,0:T(4,128)(2,1)S(1)} collective-permute-done((bf16[1,4,3,4,256]{4,3,2,1,0:T(4,128)(2,1)}, bf16[1,4,3,4,256]{4,3,2,1,0:T(4,128)(2,1)S(1)}, u32[]{:S(2)}, u32[]{:S(2)}) %collective-permute-start) | collective-permute-done | bytes 24608 | tf_op jit(solution)/shard_map/ppermute | solution.py:166
  3.6 1.3 %collective-permute-start.2 = (bf16[128,256]{1,0:T(8,128)(2,1)S(1)}, bf16[128,256]{1,0:T(8,128)(2,1)S(1)}, u32[]{:S(2)}, u32[]{:S(2)}) collective-permute-start(bf16[128,256]{1,0:T(8,128)(2,1)S(1)} %pad_maximum_fusion.refs_1_), channel_id=1, source_target_pairs={{4,0},{8,4},{12,8},{5,1},{9,5},{13,9},{6,2},{10,6},{14,10},{7,3},{... | collective-permute-start | bytes 196616 | tf_op jit(solution)/shard_map/ppermute | solution.py:169
  4.9 4.9 %collective-permute-start.1 = (bf16[128,256]{1,0:T(8,128)(2,1)S(1)}, bf16[128,256]{1,0:T(8,128)(2,1)S(1)}, u32[]{:S(2)}, u32[]{:S(2)}) collective-permute-start(bf16[128,256]{1,0:T(8,128)(2,1)S(1)} %pad_maximum_fusion.refs_1_), channel_id=1, source_target_pairs={{0,4},{4,8},{8,12},{1,5},{5,9},{9,13},{2,6},{6,10},{10,14},{3,7},{... | collective-permute-start | bytes 196616 | tf_op jit(solution)/shard_map/ppermute | solution.py:168
  10.5 0.8 %reshape.20 = bf16[64,81]{0,1:T(8,128)(2,1)S(1)} reshape(bf16[64,3,3,3,3]{0,4,3,2,1:T(4,128)(2,1)} %bitcast.16) | data formatting | bytes 20736 | tf_op jit(solution)/shard_map/reshape | solution.py:187
  11.3 0.1 copy.13.first_ref
  11.4 0.0 copy-start
  11.4 1.4 %copy-done = bf16[14,81,576]{2,1,0:T(8,128)(2,1)S(1)} copy-done((bf16[14,81,576]{2,1,0:T(8,128)(2,1)S(1)}, bf16[14,81,576]{2,1,0:T(8,128)(2,1)}, u32[]{:S(2)}) %copy-start) | copy-done | bytes 1306392
  12.8 0.0 copy-start.1
  12.8 1.0 %copy-done.1 = bf16[3,3,3,64,64]{4,3,2,1,0:T(8,128)(2,1)S(1)} copy-done((bf16[3,3,3,64,64]{4,3,2,1,0:T(8,128)(2,1)S(1)}, bf16[3,3,3,64,64]{4,3,2,1,0:T(8,128)(2,1)}, u32[]{:S(2)}) %copy-start.1) | copy-done | bytes 221208
  13.8 0.0 copy-start.3
  13.8 0.9 %copy-done.3 = bf16[3,3,64,64]{3,2,1,0:T(8,128)(2,1)S(1)} copy-done((bf16[3,3,64,64]{3,2,1,0:T(8,128)(2,1)S(1)}, bf16[3,3,64,64]{3,2,1,0:T(8,128)(2,1)}, u32[]{:S(2)}) %copy-start.3) | copy-done | bytes 73752
  14.7 0.6 %prepare.1 = (bf16[896,576]{1,0:T(8,128)(2,1)S(1)}, bf16[128,2304]{1,0:T(8,128)(2,1)S(1)}, bf16[128,960]{1,0:T(8,128)(2,1)S(1)}) custom-call(bf16[64,81]{1,0:T(8,128)(2,1)S(1)} %copy.13.first_ref, bf16[14,81,576]{2,1,0:T(8,128)(2,1)S(1)} %copy-done, bf16[27,64,64]{2,1,0:T(8,128)(2,1)S(1)} %bitcast.10, bf16[9,64,64]{2,1,0:T(8,128)(2,1)S(1)} %bitcast.11), custom_call_target="tpu_custom_call" | custom-call | tf_op jit(solution)/shard_map/prepare/pallas_call | solution.py:175
  15.3 0.0 collective-permute-done.2.refs_3_
  15.3 0.0 collective-permute-done.1.refs_2_
  15.3 0.0 copy-done.2
  15.3 4.4 %encode.1 = bf16[512,128]{1,0:T(8,128)(2,1)} custom-call(s32[1]{0:T(128)S(6)} %copy.16.refs_0_, bf16[128,256]{1,0:T(8,128)(2,1)S(1)} %pad_maximum_fusion.refs_1_, bf16[128,256]{1,0:T(8,128)(2,1)S(1)} %collective-permute-done.1.refs_2_, bf16[128,256]{1,0:T(8,128)(2,1)S(1)} %collective-permute-done.2.refs_3_, bf16[256,512]{1,0:T(8,128)(2,1)S(1)} %copy-done.2, ...), custom_call_target="tpu_custom_call" | custom-call | tf_op jit(solution)/shard_map/encode/pallas_call | solution.py:193
  (6 shorter events, 0.0 us)
Async XLA Ops:
  0.0 15.3 %copy-start.2 = (bf16[256,512]{1,0:T(8,128)(2,1)S(1)}, bf16[256,512]{1,0:T(8,128)(2,1)}, u32[]{:S(2)}) copy-start(bf16[256,512]{1,0:T(8,128)(2,1)} %constant.8.clone.refs_4_) | copy-start | bytes 786436
  0.0 3.6 %collective-permute-start = (bf16[1,4,3,4,256]{4,3,2,1,0:T(4,128)(2,1)}, bf16[1,4,3,4,256]{4,3,2,1,0:T(4,128)(2,1)S(1)}, u32[]{:S(2)}, u32[]{:S(2)}) collective-permute-start(bf16[1,4,3,4,256]{4,3,2,1,0:T(4,128)(2,1)} %param.7), channel_id=1, source_target_pairs={{0,1},{2,3},{4,5},{6,7},{8,9},{10,11},{12,13},{14,15},{16,17},{18,... | collective-permute-start | bytes 73736 | tf_op jit(solution)/shard_map/ppermute | solution.py:166
  3.6 11.7 %collective-permute-start.2 = (bf16[128,256]{1,0:T(8,128)(2,1)S(1)}, bf16[128,256]{1,0:T(8,128)(2,1)S(1)}, u32[]{:S(2)}, u32[]{:S(2)}) collective-permute-start(bf16[128,256]{1,0:T(8,128)(2,1)S(1)} %pad_maximum_fusion.refs_1_), channel_id=1, source_target_pairs={{4,0},{8,4},{12,8},{5,1},{9,5},{13,9},{6,2},{10,6},{14,10},{7,3},{... | collective-permute-start | bytes 196616 | tf_op jit(solution)/shard_map/ppermute | solution.py:169
  4.9 10.4 %collective-permute-start.1 = (bf16[128,256]{1,0:T(8,128)(2,1)S(1)}, bf16[128,256]{1,0:T(8,128)(2,1)S(1)}, u32[]{:S(2)}, u32[]{:S(2)}) collective-permute-start(bf16[128,256]{1,0:T(8,128)(2,1)S(1)} %pad_maximum_fusion.refs_1_), channel_id=1, source_target_pairs={{0,4},{4,8},{8,12},{1,5},{5,9},{9,13},{2,6},{6,10},{10,14},{3,7},{... | collective-permute-start | bytes 196616 | tf_op jit(solution)/shard_map/ppermute | solution.py:168
  11.4 1.4 %copy-start = (bf16[14,81,576]{2,1,0:T(8,128)(2,1)S(1)}, bf16[14,81,576]{2,1,0:T(8,128)(2,1)}, u32[]{:S(2)}) copy-start(bf16[14,81,576]{2,1,0:T(8,128)(2,1)} %constant.7.clone.places_ref) | copy-start | bytes 3919108
  12.8 1.0 %copy-start.1 = (bf16[3,3,3,64,64]{4,3,2,1,0:T(8,128)(2,1)S(1)}, bf16[3,3,3,64,64]{4,3,2,1,0:T(8,128)(2,1)}, u32[]{:S(2)}) copy-start(bf16[3,3,3,64,64]{4,3,2,1,0:T(8,128)(2,1)} %param.10) | copy-start | bytes 663556
  13.8 0.9 %copy-start.3 = (bf16[3,3,64,64]{3,2,1,0:T(8,128)(2,1)S(1)}, bf16[3,3,64,64]{3,2,1,0:T(8,128)(2,1)}, u32[]{:S(2)}) copy-start(bf16[3,3,64,64]{3,2,1,0:T(8,128)(2,1)} %param.11) | copy-start | bytes 221188

commit v2 on v1

v2 whole, which is shorter than its diff:
```python
import jax
import jax.numpy as jnp
from jax import lax
from jax.experimental import pallas as pl
from jax.experimental.pallas import tpu as pltpu
from jax.sharding import PartitionSpec as P

VIEWS = 4
PARITIES = 2
TAPS = 3
GROUP = 3
SLOT = 16
SUBLANES = 8

VMEM = pl.BlockSpec(memory_space=pltpu.VMEM)
HBM = pl.BlockSpec(memory_space=pltpu.HBM)
SMEM = pl.BlockSpec(memory_space=pltpu.SMEM)


def one_hot(shape, target, valid):
    lane = lax.broadcasted_iota(jnp.int32, shape, 1)
    return jnp.where(lane == jnp.where(valid, target, -1), 1.0, 0.0).astype(jnp.bfloat16)


def prepare_kernel(count, first_hbm, second_hbm, down_hbm, first_out, second_out, down_out, live_out, gather_out, columns_out, first, second, down, sems, *, rows, frames):
    arrays = ((first_hbm, first), (second_hbm, second), (down_hbm, down))
    copies = [pltpu.make_async_copy(source, target, sems.at[i]) for i, (source, target) in enumerate(arrays)]
    for copy in copies:
        copy.start()
    channels = first.shape[2]
    colors = first.shape[1]

    size = TAPS**3 * SUBLANES
    line = lax.broadcasted_iota(jnp.int32, (size, 1), 0)
    tap, color = line // SUBLANES, line % SUBLANES
    target = (tap // TAPS**2 * VIEWS + tap % TAPS) * SLOT + tap // TAPS % TAPS * colors + color
    chosen = one_hot((size, first_out.shape[1]), target, color < colors)

    width = columns_out.shape[0]
    column = lax.broadcasted_iota(jnp.int32, columns_out.shape, 0)
    place = lax.broadcasted_iota(jnp.int32, columns_out.shape, 1)
    half = width // 2
    columns_out[...] = jnp.where(column == place % half * 2 + place // half - 1, 1.0, 0.0).astype(jnp.bfloat16)

    odd = lax.rem(lax.axis_index("frames"), 2)
    groups = -(-(rows + 3) // GROUP)
    line = lax.broadcasted_iota(jnp.int32, (gather_out.shape[0], 1), 0)
    frame, group, inner = line // (groups * SLOT), line // SLOT % groups, line % SLOT
    row, color = group * GROUP + inner // colors - 3, inner % colors
    source = jnp.where(row < 0, 1 + odd, jnp.where(row < rows, 0, 2 - odd))
    local = jnp.where(row < 0, row + rows, jnp.where(row < rows, row, row - rows))
    target = ((source * (frames + 4) + frame) * colors + color) * rows + local
    gather_out[...] = one_hot(gather_out.shape, target, jnp.logical_and(inner < (GROUP + 2) * colors, row < rows + 2))

    half = live_out.shape[1] // (frames + 2)
    frame = lax.broadcasted_iota(jnp.int32, live_out.shape, 1) // half + (lax.axis_index("frames") * frames - 2)
    row = lax.broadcasted_iota(jnp.int32, live_out.shape, 0) + (lax.axis_index("rows") * rows - 2)
    inside = jnp.logical_and(row >= 0, row < lax.axis_size("rows") * rows)
    live_out[...] = jnp.where(jnp.logical_and(inside, frame < count[0]), 1.0, 0.0)

    for copy in copies:
        copy.wait()
    filler = jnp.zeros((SUBLANES - colors, channels), jnp.float32)
    lines = []
    for tap in range(TAPS**3):
        lines += [first[tap].astype(jnp.float32), filler]
    lines = jnp.concatenate(lines, axis=0).T.astype(jnp.bfloat16)
    base = jnp.dot(lines, chosen, preferred_element_type=jnp.float32)
    for block in range(GROUP):
        for parity in range(PARITIES):
            shift = parity * SLOT + block * colors
            moved = pltpu.roll(base, shift, 1) if shift else base
            start = (block * PARITIES + parity) * channels
            first_out[start:start + channels, :] = moved.astype(jnp.bfloat16)

    none = jnp.zeros((channels, channels), jnp.bfloat16)
    for tap in range(TAPS * TAPS):
        taps = [second[tap * TAPS + tap_x] for tap_x in range(TAPS)]
        columns = slice(tap * VIEWS * channels, (tap + 1) * VIEWS * channels)
        second_out[:channels, columns] = jnp.concatenate(taps + [none], axis=1)
        second_out[channels:, columns] = jnp.concatenate([none] + taps, axis=1)

    out_rows = down_out.shape[0] // channels
    sum_rows = down_out.shape[1] // (TAPS * channels)
    taps = jnp.concatenate([down[tap] for tap in range(TAPS * TAPS)], axis=1)
    place = lax.broadcasted_iota(jnp.int32, (down_out.shape[0], channels), 0)
    channel = lax.broadcasted_iota(jnp.int32, (down_out.shape[0], channels), 1)
    total = None
    for y in range(out_rows):
        spread = (place == channel * out_rows + y).astype(jnp.float32).astype(jnp.bfloat16)
        pieces = [taps]
        before, after = 2 * y, sum_rows - TAPS - 2 * y
        if before:
            pieces = [jnp.zeros((channels, before * TAPS * channels), jnp.bfloat16)] + pieces
        if after:
            pieces = pieces + [jnp.zeros((channels, after * TAPS * channels), jnp.bfloat16)]
        part = jnp.dot(spread, jnp.concatenate(pieces, axis=1), preferred_element_type=jnp.float32)
        total = part if total is None else total + part
    down_out[...] = total.astype(jnp.bfloat16)


def encode_kernel(own_ref, there_ref, back_ref, gather_ref, columns_ref, live_ref, first_w, second_w, down_w, out_ref, lines, bands, act, held, taps, *, rows, frames):
    half = columns_ref.shape[1] // VIEWS
    channels = second_w.shape[0] // PARITIES
    pair = PARITIES * channels
    wide = (frames + 2) * half
    narrow = frames * half
    groups = -(-(rows + 3) // GROUP)
    odd = lax.rem(lax.axis_index("frames"), 2)
    row_device = lax.axis_index("rows")
    top, bottom = row_device == 0, row_device == lax.axis_size("rows") - 1
    keep_there = jnp.where(jnp.logical_or(jnp.logical_and(odd == 0, top), jnp.logical_and(odd == 1, bottom)), 0.0, 1.0)
    keep_back = jnp.where(jnp.logical_or(jnp.logical_and(odd == 1, top), jnp.logical_and(odd == 0, bottom)), 0.0, 1.0)
    size = own_ref.shape[0]
    lines[:size, :] = own_ref[...]
    lines[size:2 * size, :] = (there_ref[...].astype(jnp.float32) * keep_there).astype(jnp.bfloat16)
    lines[2 * size:, :] = (back_ref[...].astype(jnp.float32) * keep_back).astype(jnp.bfloat16)
    spread = jnp.dot(gather_ref[...], lines[...], preferred_element_type=jnp.float32).astype(jnp.bfloat16)
    spread = jnp.dot(spread, columns_ref[...], preferred_element_type=jnp.float32).astype(jnp.bfloat16)
    depth = VIEWS * SLOT
    for group in range(groups):
        for view in range(VIEWS):
            place = group * depth + view * SLOT
            for t in range(frames + 4):
                source = (t * groups + group) * SLOT
                bands[place:place + SLOT, t * half:(t + 1) * half] = spread[source:source + SLOT, view * half:(view + 1) * half]

    lane = lax.broadcasted_iota(jnp.int32, (channels, half), 1)
    for row in range(rows + 3):
        group, block = row // GROUP, row % GROUP
        band = jnp.concatenate([bands[group * depth:(group + 1) * depth, tap * half:tap * half + wide] for tap in range(TAPS)], axis=0)
        total = jnp.dot(first_w[block * pair:(block + 1) * pair, :], band, preferred_element_type=jnp.float32)
        first = (total * live_ref[row:row + 1, :]).astype(jnp.bfloat16)
        if 1 <= row <= rows + 1:
            held[(row - 1) * pair:row * pair, :] = first[:, 2 * half:]
        value = first.astype(jnp.float32)
        value = value / (1 + jnp.exp(-value))
        base = row * VIEWS * channels
        act[base + channels:base + 3 * channels, :] = value.astype(jnp.bfloat16)
        for t in range(frames + 2):
            lanes = slice(t * half, (t + 1) * half)
            left = jnp.where(lane == 0, 0.0, pltpu.roll(value[channels:, lanes], 1, 1))
            right = jnp.where(lane == half - 1, 0.0, pltpu.roll(value[:channels, lanes], half - 1, 1))
            act[base:base + channels, lanes] = left.astype(jnp.bfloat16)
            act[base + 3 * channels:base + 4 * channels, lanes] = right.astype(jnp.bfloat16)

    window = TAPS * VIEWS * channels
    for row in range(rows + 1):
        base = row * VIEWS * channels
        total = None
        for tap in range(TAPS):
            part = jnp.dot(
                second_w[:, tap * window:(tap + 1) * window],
                act[base:base + window, tap * half:tap * half + narrow],
                preferred_element_type=jnp.float32,
            )
            total = part if total is None else total + part
        second = total * live_ref[row + 1:row + 2, 2 * half:]
        value = (held[row * pair:(row + 1) * pair, :].astype(jnp.float32) + second).astype(jnp.bfloat16)
        base = row * TAPS * channels
        taps[base + channels:base + 3 * channels, :] = value
        value = value.astype(jnp.float32)
        for t in range(frames):
            lanes = slice(t * half, (t + 1) * half)
            left = jnp.where(lane == 0, 0.0, pltpu.roll(value[channels:, lanes], 1, 1))
            taps[base:base + channels, lanes] = left.astype(jnp.bfloat16)
    encoded = jnp.dot(down_w[...], taps[...], preferred_element_type=jnp.float32).astype(jnp.bfloat16)
    size = down_w.shape[0]
    for t in range(frames):
        out_ref[t * size:(t + 1) * size, :] = encoded[:, t * half:(t + 1) * half]


def hbm(array):
    return pltpu.with_memory_space_constraint(array, pltpu.HBM)


def snake(row_devices, frame_devices):
    route = []
    for left in range(0, frame_devices, 2):
        ring = [(row, left) for row in range(row_devices)] + [(row, left + 1) for row in reversed(range(row_devices))]
        ring = [row * frame_devices + frame for row, frame in ring]
        route += list(zip(ring, ring[1:] + ring[:1]))
    return route


def shards(pixels, frame_counts, weight_first, weight_second, weight_down):
    clips, frames, colors, rows, width = pixels.shape
    channels = weight_first.shape[3]
    half = width // 2
    out_rows = rows // 2
    frame_devices, row_devices = lax.axis_size("frames"), lax.axis_size("rows")
    assert clips == 1 and frames >= 4 and rows >= 3 and rows % 2 == 0
    assert (GROUP + 2) * colors <= SLOT and frame_devices % 2 == 0
    bf16 = jnp.bfloat16
    frame_device = lax.axis_index("frames")
    size = frames * colors * rows
    earlier = lax.ppermute(pixels[0, -4:], "frames", [(i, (i + 1) % frame_devices) for i in range(frame_devices)])
    late = lax.optimization_barrier(pixels[0].reshape(size, width))
    earlier = earlier.reshape(4 * colors * rows, width)
    earlier = jnp.where(frame_device > 0, earlier, jnp.zeros_like(earlier))
    own = jnp.concatenate([earlier, late], axis=0)
    own, weight_first = lax.optimization_barrier((own, weight_first))
    route = snake(row_devices, frame_devices)
    axes = ("rows", "frames")
    there = lax.ppermute(own, axes, route)
    back = lax.ppermute(own, axes, [(b, a) for a, b in route])

    pair = PARITIES * channels
    wide, narrow = (frames + 2) * half, frames * half
    depth = TAPS * VIEWS * SLOT
    groups = -(-(rows + 3) // GROUP)
    first_w, second_w, down_w, live, gather, columns = pl.pallas_call(
        lambda *refs: prepare_kernel(*refs, rows=rows, frames=frames),
        name="prepare",
        compiler_params=pltpu.CompilerParams(vmem_limit_bytes=8 << 20),
        in_specs=[SMEM] + [HBM] * 3,
        out_specs=[VMEM] * 6,
        out_shape=[
            jax.ShapeDtypeStruct((GROUP * pair, depth), bf16),
            jax.ShapeDtypeStruct((pair, TAPS * TAPS * VIEWS * channels), bf16),
            jax.ShapeDtypeStruct((channels * out_rows, (rows + 1) * TAPS * channels), bf16),
            jax.ShapeDtypeStruct((rows + 3, wide), jnp.float32),
            jax.ShapeDtypeStruct(((frames + 4) * groups * SLOT, 3 * own.shape[0]), bf16),
            jax.ShapeDtypeStruct((width, VIEWS * half), bf16),
        ],
        scratch_shapes=[
            pltpu.VMEM((TAPS**3, colors, channels), bf16),
            pltpu.VMEM((TAPS**3, channels, channels), bf16),
            pltpu.VMEM((TAPS**2, channels, channels), bf16),
            pltpu.SemaphoreType.DMA((3,)),
        ],
    )(
        frame_counts,
        hbm(weight_first.transpose(0, 1, 2, 4, 3).reshape(TAPS**3, colors, channels)),
        hbm(weight_second.reshape(TAPS**3, channels, channels)),
        hbm(weight_down.reshape(TAPS**2, channels, channels)),
    )
    encoded = pl.pallas_call(
        lambda *refs: encode_kernel(*refs, rows=rows, frames=frames),
        name="encode",
        compiler_params=pltpu.CompilerParams(vmem_limit_bytes=24 << 20),
        in_specs=[VMEM] * 9,
        out_specs=VMEM,
        out_shape=jax.ShapeDtypeStruct((frames * channels * out_rows, half), bf16),
        scratch_shapes=[
            pltpu.VMEM((3 * own.shape[0], width), bf16),
            pltpu.VMEM((groups * VIEWS * SLOT, (frames + 4) * half), bf16),
            pltpu.VMEM(((rows + 3) * VIEWS * channels, wide), bf16),
            pltpu.VMEM(((rows + 1) * pair, narrow), bf16),
            pltpu.VMEM(((rows + 1) * TAPS * channels, narrow), bf16),
        ],
    )(own, there, back, gather, columns, live, first_w, second_w, down_w)
    return encoded.reshape(1, frames, channels, out_rows, half)


def solution(mesh):
    in_specs = (
        P(("groups", "clips"), "frames", None, "rows", None),
        P(("groups", "clips")),
        P(),
        P(),
        P(),
    )
    out_specs = P(("groups", "clips"), "frames", None, "rows", None)
    return jax.shard_map(shards, mesh=mesh, in_specs=in_specs, out_specs=out_specs, check_vma=False)
```

time: 20.1 us -> 11.3 us (0.56)
  the two profiles are of different devices: /device:TPU:0 before, /device:TPU:1 now
where the time goes in v2:
time: 11.3 us; the launch traced here: 11.1 us
  Pallas kernels  5.82 us (52%)
  starting transfers between devices  2.48 us (22%)
  waiting for transfers between devices  1.32 us (12%)
  local copies, waits for them, and re-layouts  0.76 us (7%)
  between operations  0.69 us (6%)
    pallas_call x1, Pallas kernels, shards(): pl.pallas_call(lambda *refs: encode_kernel(*refs, rows=rows, frames=frame...  4.23 us
    ppermute x1, starting transfers between devices, shards(): back = lax.ppermute(own, axes, [(b, a) for a, b in route])  2.46 us
    pallas_call x1, Pallas kernels, shards(): pl.pallas_call(lambda *refs: prepare_kernel(*refs, rows=rows, frames=fram...  1.59 us
    another operation x1, local copies, waits for them, and re-layouts, shards(): late = lax.optimization_barrier(pixels[0].reshape(size, width))  0.75 us
    ppermute x1, waiting for transfers between devices, shards(): there = lax.ppermute(own, axes, route)  0.68 us
    ppermute x1, waiting for transfers between devices, shards(): lax.ppermute(pixels[0, -4:], 'frames', [(i, (i + 1) % frame_devices) for...  0.63 us
  transfers between devices with their start and end apart: 3, of which 2 were waited for; matrix products, arithmetic and copies ran while one was open for 7% of the time, Pallas kernels for 14%

profile of v2, /device:TPU:1, one launch (start us, length us, event | category | flops | bytes accessed | tf_op | source)
XLA Modules:
  0.0 11.1 jit_solution(14831080780258316133)
XLA Ops:
  0.0 0.0 collective-permute-start
  0.0 0.7 %reshape_squeeze.3 = bf16[48,256]{1,0:T(8,128)(2,1)S(1)} reshape(bf16[1,4,3,4,256]{4,3,2,1,0:T(4,128)(2,1)} %param.5) | data formatting | bytes 49152 | tf_op jit(solution)/shard_map/reshape;squeeze | solution.py:198
  0.8 0.6 %collective-permute-done = bf16[4,3,4,256]{3,2,1,0:T(4,128)(2,1)S(1)} collective-permute-done((bf16[4,3,4,256]{3,2,1,0:T(4,128)(2,1)}, bf16[4,3,4,256]{3,2,1,0:T(4,128)(2,1)S(1)}, u32[]{:S(2)}, u32[]{:S(2)}) %collective-permute-start) | collective-permute-done | bytes 24608 | tf_op jit(solution)/shard_map/ppermute | solution.py:197
  1.5 2.5 %collective-permute-start.2 = (bf16[96,256]{1,0:T(8,128)(2,1)S(1)}, bf16[96,256]{1,0:T(8,128)(2,1)S(1)}, u32[]{:S(2)}, u32[]{:S(2)}) collective-permute-start(bf16[96,256]{1,0:T(8,128)(2,1)S(1)} %pad_maximum_fusion.refs_0_), channel_id=1, source_target_pairs={{4,0},{8,4},{12,8},{13,12},{9,13},{5,9},{1,5},{0,1},{6,2},{10,6},{... | collective-permute-start | bytes 147464 | tf_op jit(solution)/shard_map/ppermute | solution.py:206
  3.9 0.0 collective-permute-start.1
  4.6 1.6 %prepare.1 = (bf16[384,192]{1,0:T(8,128)(2,1)S(1)}, bf16[128,2304]{1,0:T(8,128)(2,1)S(1)}, bf16[128,960]{1,0:T(8,128)(2,1)S(1)}, f32[7,768]{1,0:T(8,128)S(1)}, b...) custom-call(s32[1]{0:T(128)S(6)} %copy.6.refs_0_, bf16[27,3,64]{2,1,0:T(4,128)(2,1)} %bitcast.9, ...), custom_call_target="tpu_custom_call" | custom-call | tf_op jit(solution)/shard_map/prepare/pallas_call | solution.py:212
  6.2 0.0 collective-permute-done.2.refs_2_
  6.2 0.7 %collective-permute-done.1.refs_1_ = bf16[96,256]{1,0:T(8,128)(2,1)S(1)} collective-permute-done((bf16[96,256]{1,0:T(8,128)(2,1)S(1)}, bf16[96,256]{1,0:T(8,128)(2,1)S(1)}, u32[]{:S(2)}, u32[]{:S(2)}) %collective-permute-start.1) | collective-permute-done | bytes 49184 | tf_op jit(solution)/shard_map/ppermute | solution.py:205
  6.9 4.2 %encode.1 = bf16[512,128]{1,0:T(8,128)(2,1)} custom-call(bf16[96,256]{1,0:T(8,128)(2,1)S(1)} %pad_maximum_fusion.refs_0_, bf16[96,256]{1,0:T(8,128)(2,1)S(1)} %collective-permute-done.1.refs_1_, bf16[96,256]{1,0:T(8,128)(2,1)S(1)} %collective-permute-done.2.refs_2_, bf16[384,288]{1,0:T(8,128)(2,1)S(1)} %get-tuple-element.15.refs_3_, ...), custom_call_target="tpu_custom_call" | custom-call | tf_op jit(solution)/shard_map/encode/pallas_call | solution.py:238
  (3 shorter events, 0.0 us)
Async XLA Ops:
  0.0 1.4 %collective-permute-start = (bf16[4,3,4,256]{3,2,1,0:T(4,128)(2,1)}, bf16[4,3,4,256]{3,2,1,0:T(4,128)(2,1)S(1)}, u32[]{:S(2)}, u32[]{:S(2)}) collective-permute-start(bf16[4,3,4,256]{3,2,1,0:T(4,128)(2,1)} %bitcast.10), channel_id=1, source_target_pairs={{0,1},{1,0},{2,3},{3,2},{4,5},{5,4},{6,7},{7,6},{8,9},{9,8},{10,11... | collective-permute-start | bytes 73736 | tf_op jit(solution)/shard_map/ppermute | solution.py:197
  1.5 4.7 %collective-permute-start.2 = (bf16[96,256]{1,0:T(8,128)(2,1)S(1)}, bf16[96,256]{1,0:T(8,128)(2,1)S(1)}, u32[]{:S(2)}, u32[]{:S(2)}) collective-permute-start(bf16[96,256]{1,0:T(8,128)(2,1)S(1)} %pad_maximum_fusion.refs_0_), channel_id=1, source_target_pairs={{4,0},{8,4},{12,8},{13,12},{9,13},{5,9},{1,5},{0,1},{6,2},{10,6},{... | collective-permute-start | bytes 147464 | tf_op jit(solution)/shard_map/ppermute | solution.py:206
  3.9 2.9 %collective-permute-start.1 = (bf16[96,256]{1,0:T(8,128)(2,1)S(1)}, bf16[96,256]{1,0:T(8,128)(2,1)S(1)}, u32[]{:S(2)}, u32[]{:S(2)}) collective-permute-start(bf16[96,256]{1,0:T(8,128)(2,1)S(1)} %pad_maximum_fusion.refs_0_), channel_id=1, source_target_pairs={{0,4},{4,8},{8,12},{12,13},{13,9},{9,5},{5,1},{1,0},{2,6},{6,10},{... | collective-permute-start | bytes 147464 | tf_op jit(solution)/shard_map/ppermute | solution.py:205

commit v3 on v2

--- a/solution.py
+++ b/solution.py
@@ -11,6 +11,7 @@
 GROUP = 3
 SLOT = 16
 SUBLANES = 8
+HALVES = 2
 
 VMEM = pl.BlockSpec(memory_space=pltpu.VMEM)
 HBM = pl.BlockSpec(memory_space=pltpu.HBM)
@@ -49,7 +50,7 @@
     row, color = group * GROUP + inner // colors - 3, inner % colors
     source = jnp.where(row < 0, 1 + odd, jnp.where(row < rows, 0, 2 - odd))
     local = jnp.where(row < 0, row + rows, jnp.where(row < rows, row, row - rows))
-    target = ((source * (frames + 4) + frame) * colors + color) * rows + local
+    target = ((source * ((frames + 4) // HALVES) + frame) * colors + color) * rows + local
     gather_out[...] = one_hot(gather_out.shape, target, jnp.logical_and(inner < (GROUP + 2) * colors, row < rows + 2))
 
     half = live_out.shape[1] // (frames + 2)
@@ -109,65 +110,101 @@
     odd = lax.rem(lax.axis_index("frames"), 2)
     row_device = lax.axis_index("rows")
     top, bottom = row_device == 0, row_device == lax.axis_size("rows") - 1
-    keep_there = jnp.where(jnp.logical_or(jnp.logical_and(odd == 0, top), jnp.logical_and(odd == 1, bottom)), 0.0, 1.0)
-    keep_back = jnp.where(jnp.logical_or(jnp.logical_and(odd == 1, top), jnp.logical_and(odd == 0, bottom)), 0.0, 1.0)
-    size = own_ref.shape[0]
-    lines[:size, :] = own_ref[...]
-    lines[size:2 * size, :] = (there_ref[...].astype(jnp.float32) * keep_there).astype(jnp.bfloat16)
-    lines[2 * size:, :] = (back_ref[...].astype(jnp.float32) * keep_back).astype(jnp.bfloat16)
-    spread = jnp.dot(gather_ref[...], lines[...], preferred_element_type=jnp.float32).astype(jnp.bfloat16)
-    spread = jnp.dot(spread, columns_ref[...], preferred_element_type=jnp.float32).astype(jnp.bfloat16)
+    keep_there = jnp.where(jnp.logical_or(jnp.logical_and(odd == 0, top), jnp.logical_and(odd == 1, bottom)), 0.0, 1.0).astype(jnp.bfloat16)
+    keep_back = jnp.where(jnp.logical_or(jnp.logical_and(odd == 1, top), jnp.logical_and(odd == 0, bottom)), 0.0, 1.0).astype(jnp.bfloat16)
+    size = own_ref.shape[0] // HALVES
+    count = (frames + 4) // HALVES
     depth = VIEWS * SLOT
+    for part in range(HALVES):
+        rows_of = slice(part * size, (part + 1) * size)
+        base = part * 3 * size
+        lines[base:base + size, :] = own_ref[rows_of, :]
+        lines[base + size:base + 2 * size, :] = there_ref[rows_of, :] * keep_there
+        lines[base + 2 * size:base + 3 * size, :] = back_ref[rows_of, :] * keep_back
+        spread = jnp.dot(gather_ref[...], lines[base:base + 3 * size, :], preferred_element_type=jnp.float32).astype(jnp.bfloat16)
+        spread = jnp.dot(spread, columns_ref[...], preferred_element_type=jnp.float32).astype(jnp.bfloat16)
+        for t in range(count):
+            lanes = slice((part * count + t) * half, (part * count + t + 1) * half)
+            for group in range(groups):
+                source = (t * groups + group) * SLOT
+                for view in range(VIEWS):
+                    place = group * depth + view * SLOT
+                    bands[place:place + SLOT, lanes] = spread[source:source + SLOT, view * half:(view + 1) * half]
+
+    lane = lax.broadcasted_iota(jnp.int32, (channels, half), 1)
+    zero = jnp.zeros((channels, half), jnp.bfloat16)
+
+    def to_right(value):
+        return jnp.where(lane == 0, zero, pltpu.roll(value, 1, 1))
+
+    def to_left(value):
+        return jnp.where(lane == half - 1, zero, pltpu.roll(value, half - 1, 1))
+
+    step = 2 * half
+
+    def first_conv(group, chunk):
+        lanes = slice(chunk * step, (chunk + 1) * step)
+        blocks = min(GROUP, rows + 3 - group * GROUP)
+        band = [bands[group * depth:(group + 1) * depth, tap * half + chunk * step:tap * half + (chunk + 1) * step] for tap in range(TAPS)]
+        total = jnp.dot(first_w[:blocks * pair, :], jnp.concatenate(band, axis=0), preferred_element_type=jnp.float32)
+        for block in range(blocks):
+            row = group * GROUP + block
+            first = total[block * pair:(block + 1) * pair, :].astype(jnp.bfloat16) * live_ref[row:row + 1, lanes].astype(jnp.bfloat16)
+            if 1 <= row <= rows + 1 and chunk > 0:
+                held[(row - 1) * pair:row * pair, (chunk - 1) * step:chunk * step] = first
+            value = 0.5 * first.astype(jnp.float32)
+            value = (value + value * jnp.tanh(value)).astype(jnp.bfloat16)
+            base = row * VIEWS * channels
+            act[base + channels:base + 3 * channels, lanes] = value
+            for t in range(2):
+                inner = slice(t * half, (t + 1) * half)
+                outer = slice(chunk * step + t * half, chunk * step + (t + 1) * half)
+                act[base:base + channels, outer] = to_right(value[channels:, inner])
+                act[base + 3 * channels:base + 4 * channels, outer] = to_left(value[:channels, inner])
+
+    window = TAPS * VIEWS * channels
+
+    def second_conv(row, chunk):
+        base = row * VIEWS * channels
+        source = [act[base:base + window, tap * half + chunk * step:tap * half + (chunk + 1) * step] for tap in range(TAPS)]
+        total = jnp.dot(second_w[...], jnp.concatenate(source, axis=0), preferred_element_type=jnp.float32)
+        second = total * live_ref[row + 1:row + 2, (chunk + 1) * step:(chunk + 2) * step]
+        lanes = slice(chunk * step, (chunk + 1) * step)
+        value = (held[row * pair:(row + 1) * pair, lanes].astype(jnp.float32) + second).astype(jnp.bfloat16)
+        base = row * TAPS * channels
+        taps[base + channels:base + 3 * channels, lanes] = value
+        for t in range(2):
+            outer = slice(chunk * step + t * half, chunk * step + (t + 1) * half)
+            taps[base:base + channels, outer] = to_right(value[channels:, t * half:(t + 1) * half])
+
+    def down_conv(chunk, first_row, last_row):
+        lanes = slice(chunk * step, (chunk + 1) * step)
+        depths = slice(first_row * TAPS * channels, last_row * TAPS * channels)
+        return jnp.dot(down_w[:, depths], taps[depths, lanes], preferred_element_type=jnp.float32)
+
+    chunks = frames // 2
+    waiting = []
     for group in range(groups):
-        for view in range(VIEWS):
-            place = group * depth + view * SLOT
-            for t in range(frames + 4):
-                source = (t * groups + group) * SLOT
-                bands[place:place + SLOT, t * half:(t + 1) * half] = spread[source:source + SLOT, view * half:(view + 1) * half]
-
-    lane = lax.broadcasted_iota(jnp.int32, (channels, half), 1)
-    for row in range(rows + 3):
-        group, block = row // GROUP, row % GROUP
-        band = jnp.concatenate([bands[group * depth:(group + 1) * depth, tap * half:tap * half + wide] for tap in range(TAPS)], axis=0)
-        total = jnp.dot(first_w[block * pair:(block + 1) * pair, :], band, preferred_element_type=jnp.float32)
-        first = (total * live_ref[row:row + 1, :]).astype(jnp.bfloat16)
-        if 1 <= row <= rows + 1:
-            held[(row - 1) * pair:row * pair, :] = first[:, 2 * half:]
-        value = first.astype(jnp.float32)
-        value = value / (1 + jnp.exp(-value))
-        base = row * VIEWS * channels
-        act[base + channels:base + 3 * channels, :] = value.astype(jnp.bfloat16)
-        for t in range(frames + 2):
-            lanes = slice(t * half, (t + 1) * half)
-            left = jnp.where(lane == 0, 0.0, pltpu.roll(value[channels:, lanes], 1, 1))
-            right = jnp.where(lane == half - 1, 0.0, pltpu.roll(value[:channels, lanes], half - 1, 1))
-            act[base:base + channels, lanes] = left.astype(jnp.bfloat16)
-            act[base + 3 * channels:base + 4 * channels, lanes] = right.astype(jnp.bfloat16)
-
-    window = TAPS * VIEWS * channels
-    for row in range(rows + 1):
-        base = row * VIEWS * channels
-        total = None
-        for tap in range(TAPS):
-            part = jnp.dot(
-                second_w[:, tap * window:(tap + 1) * window],
-                act[base:base + window, tap * half:tap * half + narrow],
-                preferred_element_type=jnp.float32,
-            )
-            total = part if total is None else total + part
-        second = total * live_ref[row + 1:row + 2, 2 * half:]
-        value = (held[row * pair:(row + 1) * pair, :].astype(jnp.float32) + second).astype(jnp.bfloat16)
-        base = row * TAPS * channels
-        taps[base + channels:base + 3 * channels, :] = value
-        value = value.astype(jnp.float32)
-        for t in range(frames):
-            lanes = slice(t * half, (t + 1) * half)
-            left = jnp.where(lane == 0, 0.0, pltpu.roll(value[channels:, lanes], 1, 1))
-            taps[base:base + channels, lanes] = left.astype(jnp.bfloat16)
-    encoded = jnp.dot(down_w[...], taps[...], preferred_element_type=jnp.float32).astype(jnp.bfloat16)
+        for chunk in range(chunks + 1):
+            first_conv(group, chunk)
+            if chunk == chunks:
+                waiting += [row for row in range(rows + 1) if group * GROUP <= row + 2 < (group + 1) * GROUP]
+            if chunk in (0, chunks) and waiting and waiting[0] < rows:
+                row = waiting.pop(0)
+                for part in range(chunks):
+                    second_conv(row, part)
+    for row in waiting[:-1]:
+        for part in range(chunks):
+            second_conv(row, part)
+    early = [down_conv(part, 0, rows) for part in range(chunks)]
+    for part in range(chunks):
+        second_conv(rows, part)
     size = down_w.shape[0]
-    for t in range(frames):
-        out_ref[t * size:(t + 1) * size, :] = encoded[:, t * half:(t + 1) * half]
+    for part in range(chunks):
+        encoded = (early[part] + down_conv(part, rows, rows + 1)).astype(jnp.bfloat16)
+        for t in range(2):
+            frame = part * 2 + t
+            out_ref[frame * size:(frame + 1) * size, :] = encoded[:, t * half:(t + 1) * half]
 
 
 def hbm(array):
@@ -199,7 +236,7 @@
     earlier = earlier.reshape(4 * colors * rows, width)
     earlier = jnp.where(frame_device > 0, earlier, jnp.zeros_like(earlier))
     own = jnp.concatenate([earlier, late], axis=0)
-    own, weight_first = lax.optimization_barrier((own, weight_first))
+    own, weight_first, frame_counts = lax.optimization_barrier((own, weight_first, frame_counts))
     route = snake(row_devices, frame_devices)
     axes = ("rows", "frames")
     there = lax.ppermute(own, axes, route)
@@ -220,7 +257,7 @@
             jax.ShapeDtypeStruct((pair, TAPS * TAPS * VIEWS * channels), bf16),
             jax.ShapeDtypeStruct((channels * out_rows, (rows + 1) * TAPS * channels), bf16),
             jax.ShapeDtypeStruct((rows + 3, wide), jnp.float32),
-            jax.ShapeDtypeStruct(((frames + 4) * groups * SLOT, 3 * own.shape[0]), bf16),
+            jax.ShapeDtypeStruct(((frames + 4) // HALVES * groups * SLOT, 3 * own.shape[0] // HALVES), bf16),
             jax.ShapeDtypeStruct((width, VIEWS * half), bf16),
         ],
         scratch_shapes=[

time: 11.3 us -> 11 us (0.973)
  Pallas kernels: 5.82 us -> 5.5 us
    pallas_call x1, Pallas kernels: 4.23 us -> 3.91 us  [shards(): pl.pallas_call(lambda *refs: encode_kernel(*refs, rows=rows, frames=frame...]
  transfers between devices with their start and end apart: 3 -> 3, of which waited for: 2 -> 2; matrix products, arithmetic and copies ran while one was open for 7% -> 7% of each run, Pallas kernels for 14% -> 15%
where the time goes in v3:
time: 11 us; the launch traced here: 10.8 us
  Pallas kernels  5.5 us (50%)
  starting transfers between devices  2.48 us (23%)
  waiting for transfers between devices  1.32 us (12%)
  local copies, waits for them, and re-layouts  0.76 us (7%)
  between operations  0.69 us (6%)
    pallas_call x1, Pallas kernels, shards(): pl.pallas_call(lambda *refs: encode_kernel(*refs, rows=rows, frames=frame...  3.91 us
    ppermute x1, starting transfers between devices, shards(): back = lax.ppermute(own, axes, [(b, a) for a, b in route])  2.46 us
    pallas_call x1, Pallas kernels, shards(): pl.pallas_call(lambda *refs: prepare_kernel(*refs, rows=rows, frames=fram...  1.59 us
    another operation x1, local copies, waits for them, and re-layouts, shards(): late = lax.optimization_barrier(pixels[0].reshape(size, width))  0.75 us
    ppermute x1, waiting for transfers between devices, shards(): there = lax.ppermute(own, axes, route)  0.68 us
    ppermute x1, waiting for transfers between devices, shards(): lax.ppermute(pixels[0, -4:], 'frames', [(i, (i + 1) % frame_devices) for...  0.63 us
  transfers between devices with their start and end apart: 3, of which 2 were waited for; matrix products, arithmetic and copies ran while one was open for 7% of the time, Pallas kernels for 15%

profile of v3, /device:TPU:1, one launch (start us, length us, event | category | flops | bytes accessed | tf_op | source)
XLA Modules:
  0.0 10.8 jit_solution(13239988046392424798)
XLA Ops:
  0.0 0.0 collective-permute-start
  0.0 0.7 %reshape_squeeze.3 = bf16[48,256]{1,0:T(8,128)(2,1)S(1)} reshape(bf16[1,4,3,4,256]{4,3,2,1,0:T(4,128)(2,1)} %param.5) | data formatting | bytes 49152 | tf_op jit(solution)/shard_map/reshape;squeeze | solution.py:235
  0.8 0.6 %collective-permute-done = bf16[4,3,4,256]{3,2,1,0:T(4,128)(2,1)S(1)} collective-permute-done((bf16[4,3,4,256]{3,2,1,0:T(4,128)(2,1)}, bf16[4,3,4,256]{3,2,1,0:T(4,128)(2,1)S(1)}, u32[]{:S(2)}, u32[]{:S(2)}) %collective-permute-start) | collective-permute-done | bytes 24608 | tf_op jit(solution)/shard_map/ppermute | solution.py:234
  1.5 2.5 %collective-permute-start.2 = (bf16[96,256]{1,0:T(8,128)(2,1)S(1)}, bf16[96,256]{1,0:T(8,128)(2,1)S(1)}, u32[]{:S(2)}, u32[]{:S(2)}) collective-permute-start(bf16[96,256]{1,0:T(8,128)(2,1)S(1)} %pad_maximum_fusion.refs_0_), channel_id=1, source_target_pairs={{4,0},{8,4},{12,8},{13,12},{9,13},{5,9},{1,5},{0,1},{6,2},{10,6},{... | collective-permute-start | bytes 147464 | tf_op jit(solution)/shard_map/ppermute | solution.py:243
  3.9 0.0 collective-permute-start.1
  4.6 1.6 %prepare.1 = (bf16[384,192]{1,0:T(8,128)(2,1)S(1)}, bf16[128,2304]{1,0:T(8,128)(2,1)S(1)}, bf16[128,960]{1,0:T(8,128)(2,1)S(1)}, f32[7,768]{1,0:T(8,128)S(1)}, b...) custom-call(s32[1]{0:T(128)S(6)} %copy.6.refs_0_, bf16[27,3,64]{2,1,0:T(4,128)(2,1)} %bitcast.9, ...), custom_call_target="tpu_custom_call" | custom-call | tf_op jit(solution)/shard_map/prepare/pallas_call | solution.py:249
  6.2 0.0 collective-permute-done.2.refs_2_
  6.2 0.7 %collective-permute-done.1.refs_1_ = bf16[96,256]{1,0:T(8,128)(2,1)S(1)} collective-permute-done((bf16[96,256]{1,0:T(8,128)(2,1)S(1)}, bf16[96,256]{1,0:T(8,128)(2,1)S(1)}, u32[]{:S(2)}, u32[]{:S(2)}) %collective-permute-start.1) | collective-permute-done | bytes 49184 | tf_op jit(solution)/shard_map/ppermute | solution.py:242
  6.9 3.9 %encode.1 = bf16[512,128]{1,0:T(8,128)(2,1)} custom-call(bf16[96,256]{1,0:T(8,128)(2,1)S(1)} %pad_maximum_fusion.refs_0_, bf16[96,256]{1,0:T(8,128)(2,1)S(1)} %collective-permute-done.1.refs_1_, bf16[96,256]{1,0:T(8,128)(2,1)S(1)} %collective-permute-done.2.refs_2_, bf16[192,144]{1,0:T(8,128)(2,1)S(1)} %get-tuple-element.17.refs_3_, ...), custom_call_target="tpu_custom_call" | custom-call | tf_op jit(solution)/shard_map/encode/pallas_call | solution.py:275
  (3 shorter events, 0.0 us)
Async XLA Ops:
  0.0 1.4 %collective-permute-start = (bf16[4,3,4,256]{3,2,1,0:T(4,128)(2,1)}, bf16[4,3,4,256]{3,2,1,0:T(4,128)(2,1)S(1)}, u32[]{:S(2)}, u32[]{:S(2)}) collective-permute-start(bf16[4,3,4,256]{3,2,1,0:T(4,128)(2,1)} %bitcast.10), channel_id=1, source_target_pairs={{0,1},{1,0},{2,3},{3,2},{4,5},{5,4},{6,7},{7,6},{8,9},{9,8},{10,11... | collective-permute-start | bytes 73736 | tf_op jit(solution)/shard_map/ppermute | solution.py:234
  1.5 4.7 %collective-permute-start.2 = (bf16[96,256]{1,0:T(8,128)(2,1)S(1)}, bf16[96,256]{1,0:T(8,128)(2,1)S(1)}, u32[]{:S(2)}, u32[]{:S(2)}) collective-permute-start(bf16[96,256]{1,0:T(8,128)(2,1)S(1)} %pad_maximum_fusion.refs_0_), channel_id=1, source_target_pairs={{4,0},{8,4},{12,8},{13,12},{9,13},{5,9},{1,5},{0,1},{6,2},{10,6},{... | collective-permute-start | bytes 147464 | tf_op jit(solution)/shard_map/ppermute | solution.py:243
  3.9 2.9 %collective-permute-start.1 = (bf16[96,256]{1,0:T(8,128)(2,1)S(1)}, bf16[96,256]{1,0:T(8,128)(2,1)S(1)}, u32[]{:S(2)}, u32[]{:S(2)}) collective-permute-start(bf16[96,256]{1,0:T(8,128)(2,1)S(1)} %pad_maximum_fusion.refs_0_), channel_id=1, source_target_pairs={{0,4},{4,8},{8,12},{12,13},{13,9},{9,5},{5,1},{1,0},{2,6},{6,10},{... | collective-permute-start | bytes 147464 | tf_op jit(solution)/shard_map/ppermute | solution.py:242

commit v4 on v3

--- a/solution.py
+++ b/solution.py
@@ -142,12 +142,14 @@
 
     step = 2 * half
 
-    def first_conv(group, chunk):
-        lanes = slice(chunk * step, (chunk + 1) * step)
+    def first_dot(group, chunk):
         blocks = min(GROUP, rows + 3 - group * GROUP)
         band = [bands[group * depth:(group + 1) * depth, tap * half + chunk * step:tap * half + (chunk + 1) * step] for tap in range(TAPS)]
-        total = jnp.dot(first_w[:blocks * pair, :], jnp.concatenate(band, axis=0), preferred_element_type=jnp.float32)
-        for block in range(blocks):
+        return jnp.dot(first_w[:blocks * pair, :], jnp.concatenate(band, axis=0), preferred_element_type=jnp.float32)
+
+    def first_rest(group, chunk, total):
+        lanes = slice(chunk * step, (chunk + 1) * step)
+        for block in range(total.shape[0] // pair):
             row = group * GROUP + block
             first = total[block * pair:(block + 1) * pair, :].astype(jnp.bfloat16) * live_ref[row:row + 1, lanes].astype(jnp.bfloat16)
             if 1 <= row <= rows + 1 and chunk > 0:
@@ -162,13 +164,14 @@
                 act[base:base + channels, outer] = to_right(value[channels:, inner])
                 act[base + 3 * channels:base + 4 * channels, outer] = to_left(value[:channels, inner])
 
-    window = TAPS * VIEWS * channels
-
-    def second_conv(row, chunk):
+    def second_dot(row, chunk):
+        window = TAPS * VIEWS * channels
         base = row * VIEWS * channels
         source = [act[base:base + window, tap * half + chunk * step:tap * half + (chunk + 1) * step] for tap in range(TAPS)]
-        total = jnp.dot(second_w[...], jnp.concatenate(source, axis=0), preferred_element_type=jnp.float32)
-        second = total * live_ref[row + 1:row + 2, (chunk + 1) * step:(chunk + 2) * step]
+        return jnp.dot(second_w[...], jnp.concatenate(source, axis=0), preferred_element_type=jnp.float32)
+
+    def second_rest(row, chunk, parts):
+        second = parts * live_ref[row + 1:row + 2, (chunk + 1) * step:(chunk + 2) * step]
         lanes = slice(chunk * step, (chunk + 1) * step)
         value = (held[row * pair:(row + 1) * pair, lanes].astype(jnp.float32) + second).astype(jnp.bfloat16)
         base = row * TAPS * channels
@@ -183,22 +186,27 @@
         return jnp.dot(down_w[:, depths], taps[depths, lanes], preferred_element_type=jnp.float32)
 
     chunks = frames // 2
-    waiting = []
-    for group in range(groups):
-        for chunk in range(chunks + 1):
-            first_conv(group, chunk)
-            if chunk == chunks:
-                waiting += [row for row in range(rows + 1) if group * GROUP <= row + 2 < (group + 1) * GROUP]
-            if chunk in (0, chunks) and waiting and waiting[0] < rows:
-                row = waiting.pop(0)
-                for part in range(chunks):
-                    second_conv(row, part)
-    for row in waiting[:-1]:
-        for part in range(chunks):
-            second_conv(row, part)
+    pieces = [(group, chunk) for group in range(groups) for chunk in range(chunks + 1)]
+    waiting, final = [], [(rows, part) for part in range(chunks)]
+    total = first_dot(*pieces[0])
+    for number, (group, chunk) in enumerate(pieces):
+        beside = waiting.pop(0) if waiting else None
+        parts = second_dot(*beside) if beside else None
+        later = first_dot(*pieces[number + 1]) if number + 1 < len(pieces) else None
+        first_rest(group, chunk, total)
+        if beside:
+            second_rest(*beside, parts)
+        total = later
+        if chunk > 0:
+            for row in range(rows):
+                if group == (row + 2) // GROUP:
+                    waiting.append((row, chunk - 1))
+    for row, part in waiting:
+        second_rest(row, part, second_dot(row, part))
     early = [down_conv(part, 0, rows) for part in range(chunks)]
-    for part in range(chunks):
-        second_conv(rows, part)
+    parts = [second_dot(*piece) for piece in final]
+    for piece, part in zip(final, parts):
+        second_rest(*piece, part)
     size = down_w.shape[0]
     for part in range(chunks):
         encoded = (early[part] + down_conv(part, rows, rows + 1)).astype(jnp.bfloat16)

time: 11 us -> 10.8 us (0.982)
  Pallas kernels: 5.5 us -> 5.35 us
    pallas_call x1, Pallas kernels: 3.91 us -> 3.76 us  [shards(): pl.pallas_call(lambda *refs: encode_kernel(*refs, rows=rows, frames=frame...]
where the time goes in v4:
time: 10.8 us; the launch traced here: 10.6 us
  Pallas kernels  5.35 us (50%)
  starting transfers between devices  2.48 us (23%)
  waiting for transfers between devices  1.32 us (12%)
  local copies, waits for them, and re-layouts  0.76 us (7%)
  between operations  0.69 us (6%)
    pallas_call x1, Pallas kernels, shards(): pl.pallas_call(lambda *refs: encode_kernel(*refs, rows=rows, frames=frame...  3.76 us
    ppermute x1, starting transfers between devices, shards(): back = lax.ppermute(own, axes, [(b, a) for a, b in route])  2.46 us
    pallas_call x1, Pallas kernels, shards(): pl.pallas_call(lambda *refs: prepare_kernel(*refs, rows=rows, frames=fram...  1.59 us
    another operation x1, local copies, waits for them, and re-layouts, shards(): late = lax.optimization_barrier(pixels[0].reshape(size, width))  0.75 us
    ppermute x1, waiting for transfers between devices, shards(): there = lax.ppermute(own, axes, route)  0.68 us
    ppermute x1, waiting for transfers between devices, shards(): lax.ppermute(pixels[0, -4:], 'frames', [(i, (i + 1) % frame_devices) for...  0.63 us
  transfers between devices with their start and end apart: 3, of which 2 were waited for; matrix products, arithmetic and copies ran while one was open for 7% of the time, Pallas kernels for 15%

profile of v4, /device:TPU:1, one launch (start us, length us, event | category | flops | bytes accessed | tf_op | source)
XLA Modules:
  0.0 10.6 jit_solution(2875727723413564202)
XLA Ops:
  0.0 0.0 collective-permute-start
  0.0 0.7 %reshape_squeeze.3 = bf16[48,256]{1,0:T(8,128)(2,1)S(1)} reshape(bf16[1,4,3,4,256]{4,3,2,1,0:T(4,128)(2,1)} %param.5) | data formatting | bytes 49152 | tf_op jit(solution)/shard_map/reshape;squeeze | solution.py:243
  0.8 0.6 %collective-permute-done = bf16[4,3,4,256]{3,2,1,0:T(4,128)(2,1)S(1)} collective-permute-done((bf16[4,3,4,256]{3,2,1,0:T(4,128)(2,1)}, bf16[4,3,4,256]{3,2,1,0:T(4,128)(2,1)S(1)}, u32[]{:S(2)}, u32[]{:S(2)}) %collective-permute-start) | collective-permute-done | bytes 24608 | tf_op jit(solution)/shard_map/ppermute | solution.py:242
  1.5 2.5 %collective-permute-start.2 = (bf16[96,256]{1,0:T(8,128)(2,1)S(1)}, bf16[96,256]{1,0:T(8,128)(2,1)S(1)}, u32[]{:S(2)}, u32[]{:S(2)}) collective-permute-start(bf16[96,256]{1,0:T(8,128)(2,1)S(1)} %pad_maximum_fusion.refs_0_), channel_id=1, source_target_pairs={{4,0},{8,4},{12,8},{13,12},{9,13},{5,9},{1,5},{0,1},{6,2},{10,6},{... | collective-permute-start | bytes 147464 | tf_op jit(solution)/shard_map/ppermute | solution.py:251
  3.9 0.0 collective-permute-start.1
  4.6 1.6 %prepare.1 = (bf16[384,192]{1,0:T(8,128)(2,1)S(1)}, bf16[128,2304]{1,0:T(8,128)(2,1)S(1)}, bf16[128,960]{1,0:T(8,128)(2,1)S(1)}, f32[7,768]{1,0:T(8,128)S(1)}, b...) custom-call(s32[1]{0:T(128)S(6)} %copy.6.refs_0_, bf16[27,3,64]{2,1,0:T(4,128)(2,1)} %bitcast.9, ...), custom_call_target="tpu_custom_call" | custom-call | tf_op jit(solution)/shard_map/prepare/pallas_call | solution.py:257
  6.2 0.0 collective-permute-done.2.refs_2_
  6.2 0.7 %collective-permute-done.1.refs_1_ = bf16[96,256]{1,0:T(8,128)(2,1)S(1)} collective-permute-done((bf16[96,256]{1,0:T(8,128)(2,1)S(1)}, bf16[96,256]{1,0:T(8,128)(2,1)S(1)}, u32[]{:S(2)}, u32[]{:S(2)}) %collective-permute-start.1) | collective-permute-done | bytes 49184 | tf_op jit(solution)/shard_map/ppermute | solution.py:250
  6.9 3.8 %encode.1 = bf16[512,128]{1,0:T(8,128)(2,1)} custom-call(bf16[96,256]{1,0:T(8,128)(2,1)S(1)} %pad_maximum_fusion.refs_0_, bf16[96,256]{1,0:T(8,128)(2,1)S(1)} %collective-permute-done.1.refs_1_, bf16[96,256]{1,0:T(8,128)(2,1)S(1)} %collective-permute-done.2.refs_2_, bf16[192,144]{1,0:T(8,128)(2,1)S(1)} %get-tuple-element.17.refs_3_, ...), custom_call_target="tpu_custom_call" | custom-call | tf_op jit(solution)/shard_map/encode/pallas_call | solution.py:283
  (3 shorter events, 0.0 us)
Async XLA Ops:
  0.0 1.4 %collective-permute-start = (bf16[4,3,4,256]{3,2,1,0:T(4,128)(2,1)}, bf16[4,3,4,256]{3,2,1,0:T(4,128)(2,1)S(1)}, u32[]{:S(2)}, u32[]{:S(2)}) collective-permute-start(bf16[4,3,4,256]{3,2,1,0:T(4,128)(2,1)} %bitcast.10), channel_id=1, source_target_pairs={{0,1},{1,0},{2,3},{3,2},{4,5},{5,4},{6,7},{7,6},{8,9},{9,8},{10,11... | collective-permute-start | bytes 73736 | tf_op jit(solution)/shard_map/ppermute | solution.py:242
  1.5 4.7 %collective-permute-start.2 = (bf16[96,256]{1,0:T(8,128)(2,1)S(1)}, bf16[96,256]{1,0:T(8,128)(2,1)S(1)}, u32[]{:S(2)}, u32[]{:S(2)}) collective-permute-start(bf16[96,256]{1,0:T(8,128)(2,1)S(1)} %pad_maximum_fusion.refs_0_), channel_id=1, source_target_pairs={{4,0},{8,4},{12,8},{13,12},{9,13},{5,9},{1,5},{0,1},{6,2},{10,6},{... | collective-permute-start | bytes 147464 | tf_op jit(solution)/shard_map/ppermute | solution.py:251
  3.9 2.9 %collective-permute-start.1 = (bf16[96,256]{1,0:T(8,128)(2,1)S(1)}, bf16[96,256]{1,0:T(8,128)(2,1)S(1)}, u32[]{:S(2)}, u32[]{:S(2)}) collective-permute-start(bf16[96,256]{1,0:T(8,128)(2,1)S(1)} %pad_maximum_fusion.refs_0_), channel_id=1, source_target_pairs={{0,4},{4,8},{8,12},{12,13},{13,9},{9,5},{5,1},{1,0},{2,6},{6,10},{... | collective-permute-start | bytes 147464 | tf_op jit(solution)/shard_map/ppermute | solution.py:250

commit v5 on v4

--- a/solution.py
+++ b/solution.py
@@ -104,8 +104,6 @@
     half = columns_ref.shape[1] // VIEWS
     channels = second_w.shape[0] // PARITIES
     pair = PARITIES * channels
-    wide = (frames + 2) * half
-    narrow = frames * half
     groups = -(-(rows + 3) // GROUP)
     odd = lax.rem(lax.axis_index("frames"), 2)
     row_device = lax.axis_index("rows")
@@ -124,12 +122,11 @@
         spread = jnp.dot(gather_ref[...], lines[base:base + 3 * size, :], preferred_element_type=jnp.float32).astype(jnp.bfloat16)
         spread = jnp.dot(spread, columns_ref[...], preferred_element_type=jnp.float32).astype(jnp.bfloat16)
         for t in range(count):
-            lanes = slice((part * count + t) * half, (part * count + t + 1) * half)
             for group in range(groups):
                 source = (t * groups + group) * SLOT
                 for view in range(VIEWS):
                     place = group * depth + view * SLOT
-                    bands[place:place + SLOT, lanes] = spread[source:source + SLOT, view * half:(view + 1) * half]
+                    bands[part * count + t, place:place + SLOT, :] = spread[source:source + SLOT, view * half:(view + 1) * half]
 
     lane = lax.broadcasted_iota(jnp.int32, (channels, half), 1)
     zero = jnp.zeros((channels, half), jnp.bfloat16)
@@ -142,9 +139,12 @@
 
     step = 2 * half
 
+    def two_frames(ref, frame, rows_of):
+        return jnp.concatenate([ref[frame, rows_of, :], ref[frame + 1, rows_of, :]], axis=1)
+
     def first_dot(group, chunk):
         blocks = min(GROUP, rows + 3 - group * GROUP)
-        band = [bands[group * depth:(group + 1) * depth, tap * half + chunk * step:tap * half + (chunk + 1) * step] for tap in range(TAPS)]
+        band = [two_frames(bands, 2 * chunk + tap, slice(group * depth, (group + 1) * depth)) for tap in range(TAPS)]
         return jnp.dot(first_w[:blocks * pair, :], jnp.concatenate(band, axis=0), preferred_element_type=jnp.float32)
 
     def first_rest(group, chunk, total):
@@ -152,38 +152,37 @@
         for block in range(total.shape[0] // pair):
             row = group * GROUP + block
             first = total[block * pair:(block + 1) * pair, :].astype(jnp.bfloat16) * live_ref[row:row + 1, lanes].astype(jnp.bfloat16)
-            if 1 <= row <= rows + 1 and chunk > 0:
-                held[(row - 1) * pair:row * pair, (chunk - 1) * step:chunk * step] = first
             value = 0.5 * first.astype(jnp.float32)
             value = (value + value * jnp.tanh(value)).astype(jnp.bfloat16)
             base = row * VIEWS * channels
-            act[base + channels:base + 3 * channels, lanes] = value
             for t in range(2):
                 inner = slice(t * half, (t + 1) * half)
-                outer = slice(chunk * step + t * half, chunk * step + (t + 1) * half)
-                act[base:base + channels, outer] = to_right(value[channels:, inner])
-                act[base + 3 * channels:base + 4 * channels, outer] = to_left(value[:channels, inner])
+                if 1 <= row <= rows + 1 and chunk > 0:
+                    held[2 * (chunk - 1) + t, (row - 1) * pair:row * pair, :] = first[:, inner]
+                frame = 2 * chunk + t
+                act[frame, base:base + channels, :] = to_right(value[channels:, inner])
+                act[frame, base + channels:base + 3 * channels, :] = value[:, inner]
+                act[frame, base + 3 * channels:base + 4 * channels, :] = to_left(value[:channels, inner])
 
     def second_dot(row, chunk):
         window = TAPS * VIEWS * channels
         base = row * VIEWS * channels
-        source = [act[base:base + window, tap * half + chunk * step:tap * half + (chunk + 1) * step] for tap in range(TAPS)]
+        source = [two_frames(act, 2 * chunk + tap, slice(base, base + window)) for tap in range(TAPS)]
         return jnp.dot(second_w[...], jnp.concatenate(source, axis=0), preferred_element_type=jnp.float32)
 
     def second_rest(row, chunk, parts):
         second = parts * live_ref[row + 1:row + 2, (chunk + 1) * step:(chunk + 2) * step]
-        lanes = slice(chunk * step, (chunk + 1) * step)
-        value = (held[row * pair:(row + 1) * pair, lanes].astype(jnp.float32) + second).astype(jnp.bfloat16)
+        first = two_frames(held, 2 * chunk, slice(row * pair, (row + 1) * pair))
+        value = (first.astype(jnp.float32) + second).astype(jnp.bfloat16)
         base = row * TAPS * channels
-        taps[base + channels:base + 3 * channels, lanes] = value
         for t in range(2):
-            outer = slice(chunk * step + t * half, chunk * step + (t + 1) * half)
-            taps[base:base + channels, outer] = to_right(value[channels:, t * half:(t + 1) * half])
+            inner = slice(t * half, (t + 1) * half)
+            taps[2 * chunk + t, base:base + channels, :] = to_right(value[channels:, inner])
+            taps[2 * chunk + t, base + channels:base + 3 * channels, :] = value[:, inner]
 
     def down_conv(chunk, first_row, last_row):
-        lanes = slice(chunk * step, (chunk + 1) * step)
         depths = slice(first_row * TAPS * channels, last_row * TAPS * channels)
-        return jnp.dot(down_w[:, depths], taps[depths, lanes], preferred_element_type=jnp.float32)
+        return jnp.dot(down_w[:, depths], two_frames(taps, 2 * chunk, depths), preferred_element_type=jnp.float32)
 
     chunks = frames // 2
     pieces = [(group, chunk) for group in range(groups) for chunk in range(chunks + 1)]
@@ -234,7 +233,7 @@
     half = width // 2
     out_rows = rows // 2
     frame_devices, row_devices = lax.axis_size("frames"), lax.axis_size("rows")
-    assert clips == 1 and frames >= 4 and rows >= 3 and rows % 2 == 0
+    assert clips == 1 and frames >= 4 and rows >= 3 and rows % 2 == 0 and frames % 2 == 0
     assert (GROUP + 2) * colors <= SLOT and frame_devices % 2 == 0
     bf16 = jnp.bfloat16
     frame_device = lax.axis_index("frames")
@@ -251,7 +250,7 @@
     back = lax.ppermute(own, axes, [(b, a) for a, b in route])
 
     pair = PARITIES * channels
-    wide, narrow = (frames + 2) * half, frames * half
+    wide = (frames + 2) * half
     depth = TAPS * VIEWS * SLOT
     groups = -(-(rows + 3) // GROUP)
     first_w, second_w, down_w, live, gather, columns = pl.pallas_call(
@@ -289,10 +288,10 @@
         out_shape=jax.ShapeDtypeStruct((frames * channels * out_rows, half), bf16),
         scratch_shapes=[
             pltpu.VMEM((3 * own.shape[0], width), bf16),
-            pltpu.VMEM((groups * VIEWS * SLOT, (frames + 4) * half), bf16),
-            pltpu.VMEM(((rows + 3) * VIEWS * channels, wide), bf16),
-            pltpu.VMEM(((rows + 1) * pair, narrow), bf16),
-            pltpu.VMEM(((rows + 1) * TAPS * channels, narrow), bf16),
+            pltpu.VMEM((frames + 4, groups * VIEWS * SLOT, half), bf16),
+            pltpu.VMEM((frames + 2, (rows + 3) * VIEWS * channels, half), bf16),
+            pltpu.VMEM((frames, (rows + 1) * pair, half), bf16),
+            pltpu.VMEM((frames, (rows + 1) * TAPS * channels, half), bf16),
         ],
     )(own, there, back, gather, columns, live, first_w, second_w, down_w)
     return encoded.reshape(1, frames, channels, out_rows, half)

time: 10.8 us -> 10.8 us (level)
  no operation moved by 1% of the time
where the time goes in v5:
time: 10.8 us; the launch traced here: 10.6 us
  Pallas kernels  5.33 us (49%)
  starting transfers between devices  2.48 us (23%)
  waiting for transfers between devices  1.32 us (12%)
  local copies, waits for them, and re-layouts  0.76 us (7%)
  between operations  0.69 us (6%)
    pallas_call x1, Pallas kernels, shards(): pl.pallas_call(lambda *refs: encode_kernel(*refs, rows=rows, frames=frame...  3.74 us
    ppermute x1, starting transfers between devices, shards(): back = lax.ppermute(own, axes, [(b, a) for a, b in route])  2.46 us
    pallas_call x1, Pallas kernels, shards(): pl.pallas_call(lambda *refs: prepare_kernel(*refs, rows=rows, frames=fram...  1.59 us
    another operation x1, local copies, waits for them, and re-layouts, shards(): late = lax.optimization_barrier(pixels[0].reshape(size, width))  0.75 us
    ppermute x1, waiting for transfers between devices, shards(): there = lax.ppermute(own, axes, route)  0.68 us
    ppermute x1, waiting for transfers between devices, shards(): lax.ppermute(pixels[0, -4:], 'frames', [(i, (i + 1) % frame_devices) for...  0.63 us
  transfers between devices with their start and end apart: 3, of which 2 were waited for; matrix products, arithmetic and copies ran while one was open for 7% of the time, Pallas kernels for 15%

profile of v5, /device:TPU:1, one launch (start us, length us, event | category | flops | bytes accessed | tf_op | source)
XLA Modules:
  0.0 10.6 jit_solution(2403081718115210380)
XLA Ops:
  0.0 0.0 collective-permute-start
  0.0 0.7 %reshape_squeeze.3 = bf16[48,256]{1,0:T(8,128)(2,1)S(1)} reshape(bf16[1,4,3,4,256]{4,3,2,1,0:T(4,128)(2,1)} %param.5) | data formatting | bytes 49152 | tf_op jit(solution)/shard_map/reshape;squeeze | solution.py:242
  0.8 0.6 %collective-permute-done = bf16[4,3,4,256]{3,2,1,0:T(4,128)(2,1)S(1)} collective-permute-done((bf16[4,3,4,256]{3,2,1,0:T(4,128)(2,1)}, bf16[4,3,4,256]{3,2,1,0:T(4,128)(2,1)S(1)}, u32[]{:S(2)}, u32[]{:S(2)}) %collective-permute-start) | collective-permute-done | bytes 24608 | tf_op jit(solution)/shard_map/ppermute | solution.py:241
  1.5 2.5 %collective-permute-start.2 = (bf16[96,256]{1,0:T(8,128)(2,1)S(1)}, bf16[96,256]{1,0:T(8,128)(2,1)S(1)}, u32[]{:S(2)}, u32[]{:S(2)}) collective-permute-start(bf16[96,256]{1,0:T(8,128)(2,1)S(1)} %pad_maximum_fusion.refs_0_), channel_id=1, source_target_pairs={{4,0},{8,4},{12,8},{13,12},{9,13},{5,9},{1,5},{0,1},{6,2},{10,6},{... | collective-permute-start | bytes 147464 | tf_op jit(solution)/shard_map/ppermute | solution.py:250
  3.9 0.0 collective-permute-start.1
  4.6 1.6 %prepare.1 = (bf16[384,192]{1,0:T(8,128)(2,1)S(1)}, bf16[128,2304]{1,0:T(8,128)(2,1)S(1)}, bf16[128,960]{1,0:T(8,128)(2,1)S(1)}, f32[7,768]{1,0:T(8,128)S(1)}, b...) custom-call(s32[1]{0:T(128)S(6)} %copy.6.refs_0_, bf16[27,3,64]{2,1,0:T(4,128)(2,1)} %bitcast.9, ...), custom_call_target="tpu_custom_call" | custom-call | tf_op jit(solution)/shard_map/prepare/pallas_call | solution.py:256
  6.2 0.0 collective-permute-done.2.refs_2_
  6.2 0.7 %collective-permute-done.1.refs_1_ = bf16[96,256]{1,0:T(8,128)(2,1)S(1)} collective-permute-done((bf16[96,256]{1,0:T(8,128)(2,1)S(1)}, bf16[96,256]{1,0:T(8,128)(2,1)S(1)}, u32[]{:S(2)}, u32[]{:S(2)}) %collective-permute-start.1) | collective-permute-done | bytes 49184 | tf_op jit(solution)/shard_map/ppermute | solution.py:249
  6.9 3.7 %encode.1 = bf16[512,128]{1,0:T(8,128)(2,1)} custom-call(bf16[96,256]{1,0:T(8,128)(2,1)S(1)} %pad_maximum_fusion.refs_0_, bf16[96,256]{1,0:T(8,128)(2,1)S(1)} %collective-permute-done.1.refs_1_, bf16[96,256]{1,0:T(8,128)(2,1)S(1)} %collective-permute-done.2.refs_2_, bf16[192,144]{1,0:T(8,128)(2,1)S(1)} %get-tuple-element.17.refs_3_, ...), custom_call_target="tpu_custom_call" | custom-call | tf_op jit(solution)/shard_map/encode/pallas_call | solution.py:282
  (3 shorter events, 0.0 us)
Async XLA Ops:
  0.0 1.4 %collective-permute-start = (bf16[4,3,4,256]{3,2,1,0:T(4,128)(2,1)}, bf16[4,3,4,256]{3,2,1,0:T(4,128)(2,1)S(1)}, u32[]{:S(2)}, u32[]{:S(2)}) collective-permute-start(bf16[4,3,4,256]{3,2,1,0:T(4,128)(2,1)} %bitcast.10), channel_id=1, source_target_pairs={{0,1},{1,0},{2,3},{3,2},{4,5},{5,4},{6,7},{7,6},{8,9},{9,8},{10,11... | collective-permute-start | bytes 73736 | tf_op jit(solution)/shard_map/ppermute | solution.py:241
  1.5 4.7 %collective-permute-start.2 = (bf16[96,256]{1,0:T(8,128)(2,1)S(1)}, bf16[96,256]{1,0:T(8,128)(2,1)S(1)}, u32[]{:S(2)}, u32[]{:S(2)}) collective-permute-start(bf16[96,256]{1,0:T(8,128)(2,1)S(1)} %pad_maximum_fusion.refs_0_), channel_id=1, source_target_pairs={{4,0},{8,4},{12,8},{13,12},{9,13},{5,9},{1,5},{0,1},{6,2},{10,6},{... | collective-permute-start | bytes 147464 | tf_op jit(solution)/shard_map/ppermute | solution.py:250
  3.9 2.9 %collective-permute-start.1 = (bf16[96,256]{1,0:T(8,128)(2,1)S(1)}, bf16[96,256]{1,0:T(8,128)(2,1)S(1)}, u32[]{:S(2)}, u32[]{:S(2)}) collective-permute-start(bf16[96,256]{1,0:T(8,128)(2,1)S(1)} %pad_maximum_fusion.refs_0_), channel_id=1, source_target_pairs={{0,4},{4,8},{8,12},{12,13},{13,9},{9,5},{5,1},{1,0},{2,6},{6,10},{... | collective-permute-start | bytes 147464 | tf_op jit(solution)/shard_map/ppermute | solution.py:249

commit v6 on v5

v6 whole, which is shorter than its diff:
```python
import jax
import jax.numpy as jnp
from jax import lax
from jax.experimental import pallas as pl
from jax.experimental.pallas import tpu as pltpu
from jax.sharding import PartitionSpec as P

VIEWS = 4
PARITIES = 2
TAPS = 3
GROUP = 3
SLOT = 16
SUBLANES = 8
HALVES = 2

VMEM = pl.BlockSpec(memory_space=pltpu.VMEM)
HBM = pl.BlockSpec(memory_space=pltpu.HBM)
SMEM = pl.BlockSpec(memory_space=pltpu.SMEM)


def one_hot(shape, target, valid):
    lane = lax.broadcasted_iota(jnp.int32, shape, 1)
    return jnp.where(lane == jnp.where(valid, target, -1), 1.0, 0.0).astype(jnp.bfloat16)


def act_groups(rows):
    apart = [(0, 3), (rows + 1, 2)]
    alone = [(start, min(GROUP, rows + 1 - start)) for start in range(3, rows + 1, GROUP)]
    return apart, alone


def band_targets(size, runs, colors):
    line = lax.broadcasted_iota(jnp.int32, (size, 1), 0)
    frame, run, inner = line // (len(runs) * SLOT), line // SLOT % len(runs), line % SLOT
    start, count = 0, 0
    for number, (first, rows_of) in enumerate(runs):
        start, count = jnp.where(run == number, first, start), jnp.where(run == number, rows_of + 2, count)
    return frame, inner % colors, start + inner // colors - 3, inner < count * colors


def spread_bands(gather, lines, columns, bands, first_frame, runs):
    spread = jnp.dot(gather, lines, preferred_element_type=jnp.float32).astype(jnp.bfloat16)
    spread = jnp.dot(spread, columns, preferred_element_type=jnp.float32).astype(jnp.bfloat16)
    half = bands.shape[2]
    for line in range(spread.shape[0] // SLOT):
        t, run = line // len(runs), line % len(runs)
        for view in range(VIEWS):
            place = (run * VIEWS + view) * SLOT
            bands[first_frame + t, place:place + SLOT, :] = spread[line * SLOT:(line + 1) * SLOT, view * half:(view + 1) * half]


def tap_rows(row, rows, alone):
    return [tap for tap in range(TAPS) if (3 <= row + tap <= rows) == alone]


def second_product(weights, row_source, row, chunk, row_taps):
    channels = weights.shape[0] // PARITIES
    size = VIEWS * channels
    lines, columns = [], []
    for tap_t in range(TAPS):
        for tap_y in row_taps:
            ref, line = row_source(row + tap_y)
            lines.append(two_frames(ref, 2 * chunk + tap_t, slice(line * size, (line + 1) * size)))
            start = (tap_t * TAPS + tap_y) * size
            columns.append(weights[:, start:start + size])
    return jnp.dot(jnp.concatenate(columns, axis=1), jnp.concatenate(lines, axis=0), preferred_element_type=jnp.float32)


def two_frames(ref, frame, rows_of):
    return jnp.concatenate([ref[frame, rows_of, :], ref[frame + 1, rows_of, :]], axis=1)


def to_right(value):
    lane = lax.broadcasted_iota(jnp.int32, value.shape, 1)
    return jnp.where(lane == 0, jnp.zeros_like(value), pltpu.roll(value, 1, 1))


def to_left(value):
    lane = lax.broadcasted_iota(jnp.int32, value.shape, 1)
    return jnp.where(lane == value.shape[1] - 1, jnp.zeros_like(value), pltpu.roll(value, value.shape[1] - 1, 1))


def first_product(weights, bands, run, count, chunk):
    depth = VIEWS * SLOT
    band = [two_frames(bands, 2 * chunk + tap, slice(run * depth, (run + 1) * depth)) for tap in range(TAPS)]
    pair = weights.shape[0] // GROUP
    return jnp.dot(weights[:count * pair, :], jnp.concatenate(band, axis=0), preferred_element_type=jnp.float32)


def activate(total, live, rows_of, chunk, act, held, base_row, rows):
    half = act.shape[2]
    pair = total.shape[0] // len(rows_of)
    channels = pair // PARITIES
    for block, row in enumerate(rows_of):
        mask = live[row:row + 1, 2 * chunk * half:2 * (chunk + 1) * half].astype(jnp.bfloat16)
        first = total[block * pair:(block + 1) * pair, :].astype(jnp.bfloat16) * mask
        value = 0.5 * first.astype(jnp.float32)
        value = (value + value * jnp.tanh(value)).astype(jnp.bfloat16)
        base = (row - base_row) * VIEWS * channels
        for t in range(2):
            inner = slice(t * half, (t + 1) * half)
            if 1 <= row <= rows + 1 and chunk > 0:
                held[2 * (chunk - 1) + t, (row - base_row) * pair:(row - base_row + 1) * pair, :] = first[:, inner]
            frame = 2 * chunk + t
            act[frame, base:base + channels, :] = to_right(value[channels:, inner])
            act[frame, base + channels:base + 3 * channels, :] = value[:, inner]
            act[frame, base + 3 * channels:base + 4 * channels, :] = to_left(value[:channels, inner])


def load_kernel(*refs):
    count = (len(refs) - 1) // 2
    copies = [pltpu.make_async_copy(refs[i], refs[count + i], refs[-1].at[i]) for i in range(count)]
    for copy in copies:
        copy.start()
    for copy in copies:
        copy.wait()


def prepare_kernel(count, own, first, second, down, first_out, second_out, down_out, live_out, gather_out, columns_out, held_out, partial_out, bands, act, *, rows, frames):
    channels = first.shape[2]
    colors = first.shape[1]
    apart, alone = act_groups(rows)

    size = TAPS**3 * SUBLANES
    line = lax.broadcasted_iota(jnp.int32, (size, 1), 0)
    tap, color = line // SUBLANES, line % SUBLANES
    target = (tap // TAPS**2 * VIEWS + tap % TAPS) * SLOT + tap // TAPS % TAPS * colors + color
    chosen = one_hot((size, first_out.shape[1]), target, color < colors)

    width = columns_out.shape[0]
    column = lax.broadcasted_iota(jnp.int32, columns_out.shape, 0)
    place = lax.broadcasted_iota(jnp.int32, columns_out.shape, 1)
    half = width // 2
    columns_out[...] = jnp.where(column == place % half * 2 + place // half - 1, 1.0, 0.0).astype(jnp.bfloat16)

    part = (frames + 4) // HALVES
    size = part * colors * rows
    frame, color, row, used = band_targets(part * len(alone) * SLOT, alone, colors)
    gather = one_hot((part * len(alone) * SLOT, size), (frame * colors + color) * rows + row, used)
    for number in range(HALVES):
        spread_bands(gather, own[number * size:(number + 1) * size, :], columns_out[...], bands, number * part, alone)

    frame = lax.broadcasted_iota(jnp.int32, live_out.shape, 1) // half + (lax.axis_index("frames") * frames - 2)
    row = lax.broadcasted_iota(jnp.int32, live_out.shape, 0) + (lax.axis_index("rows") * rows - 2)
    inside = jnp.logical_and(row >= 0, row < lax.axis_size("rows") * rows)
    live_out[...] = jnp.where(jnp.logical_and(inside, frame < count[0]), 1.0, 0.0)

    filler = jnp.zeros((SUBLANES - colors, channels), jnp.float32)
    lines = []
    for tap in range(TAPS**3):
        lines += [first[tap].astype(jnp.float32), filler]
    lines = jnp.concatenate(lines, axis=0).T.astype(jnp.bfloat16)
    base = jnp.dot(lines, chosen, preferred_element_type=jnp.float32)
    for block in range(GROUP):
        for parity in range(PARITIES):
            shift = parity * SLOT + block * colors
            moved = pltpu.roll(base, shift, 1) if shift else base
            start = (block * PARITIES + parity) * channels
            first_out[start:start + channels, :] = moved.astype(jnp.bfloat16)

    for run, (start, rows_of) in enumerate(alone):
        for chunk in range(frames // 2 + 1):
            total = first_product(first_out, bands, run, rows_of, chunk)
            activate(total, live_out, range(start, start + rows_of), chunk, act, held_out, 3, rows)

    odd = lax.rem(lax.axis_index("frames"), 2)
    frame, color, row, used = band_targets(gather_out.shape[0], apart, colors)
    source = jnp.where(row < 0, 1 + odd, jnp.where(row < rows, 0, 2 - odd))
    local = jnp.where(row < 0, row + rows, jnp.where(row < rows, row, row - rows))
    gather_out[...] = one_hot(gather_out.shape, ((source * part + frame) * colors + color) * rows + local, used)

    none = jnp.zeros((channels, channels), jnp.bfloat16)
    for tap in range(TAPS * TAPS):
        taps = [second[tap * TAPS + tap_x] for tap_x in range(TAPS)]
        columns = slice(tap * VIEWS * channels, (tap + 1) * VIEWS * channels)
        second_out[:channels, columns] = jnp.concatenate(taps + [none], axis=1)
        second_out[channels:, columns] = jnp.concatenate([none] + taps, axis=1)

    for row in range(1, rows + 1):
        for chunk in range(frames // 2):
            partial_out[row - 1, chunk] = second_product(second_out, lambda line: (act, line - 3), row, chunk, tap_rows(row, rows, True))

    out_rows = down_out.shape[0] // channels
    sum_rows = down_out.shape[1] // (TAPS * channels)
    taps = jnp.concatenate([down[tap] for tap in range(TAPS * TAPS)], axis=1)
    place = lax.broadcasted_iota(jnp.int32, (down_out.shape[0], channels), 0)
    channel = lax.broadcasted_iota(jnp.int32, (down_out.shape[0], channels), 1)
    total = None
    for y in range(out_rows):
        spread = (place == channel * out_rows + y).astype(jnp.float32).astype(jnp.bfloat16)
        pieces = [taps]
        before, after = 2 * y, sum_rows - TAPS - 2 * y
        if before:
            pieces = [jnp.zeros((channels, before * TAPS * channels), jnp.bfloat16)] + pieces
        if after:
            pieces = pieces + [jnp.zeros((channels, after * TAPS * channels), jnp.bfloat16)]
        part = jnp.dot(spread, jnp.concatenate(pieces, axis=1), preferred_element_type=jnp.float32)
        total = part if total is None else total + part
    down_out[...] = total.astype(jnp.bfloat16)


def encode_kernel(own_ref, there_ref, back_ref, gather_ref, columns_ref, live_ref, held_own, partial_ref, first_w, second_w, down_w, out_ref, lines, bands, act, held, taps, *, rows, frames):
    half = columns_ref.shape[1] // VIEWS
    channels = second_w.shape[0] // PARITIES
    pair = PARITIES * channels
    apart, _ = act_groups(rows)
    odd = lax.rem(lax.axis_index("frames"), 2)
    row_device = lax.axis_index("rows")
    top, bottom = row_device == 0, row_device == lax.axis_size("rows") - 1
    keep_there = jnp.where(jnp.logical_or(jnp.logical_and(odd == 0, top), jnp.logical_and(odd == 1, bottom)), 0.0, 1.0).astype(jnp.bfloat16)
    keep_back = jnp.where(jnp.logical_or(jnp.logical_and(odd == 1, top), jnp.logical_and(odd == 0, bottom)), 0.0, 1.0).astype(jnp.bfloat16)
    size = own_ref.shape[0] // HALVES
    for part in range(HALVES):
        rows_of = slice(part * size, (part + 1) * size)
        base = part * 3 * size
        lines[base:base + size, :] = own_ref[rows_of, :]
        lines[base + size:base + 2 * size, :] = there_ref[rows_of, :] * keep_there
        lines[base + 2 * size:base + 3 * size, :] = back_ref[rows_of, :] * keep_back
        spread_bands(gather_ref[...], lines[base:base + 3 * size, :], columns_ref[...], bands, part * (frames + 4) // HALVES, apart)

    step = 2 * half
    chunks = frames // 2

    def second_dot(row, chunk):
        total = second_product(second_w, lambda line: (act, line), row, chunk, tap_rows(row, rows, False))
        return total + partial_ref[row - 1, chunk] if row > 0 else total

    def second_rest(row, chunk, total):
        second = total * live_ref[row + 1:row + 2, (chunk + 1) * step:(chunk + 2) * step]
        source, base = (held_own, row - 2) if 3 <= row + 1 <= rows else (held, row + 1)
        first = two_frames(source, 2 * chunk, slice(base * pair, (base + 1) * pair))
        value = (first.astype(jnp.float32) + second).astype(jnp.bfloat16)
        base = row * TAPS * channels
        for t in range(2):
            inner = slice(t * half, (t + 1) * half)
            taps[2 * chunk + t, base:base + channels, :] = to_right(value[channels:, inner])
            taps[2 * chunk + t, base + channels:base + 3 * channels, :] = value[:, inner]

    def down_conv(chunk, first_row, last_row):
        depths = slice(first_row * TAPS * channels, last_row * TAPS * channels)
        return jnp.dot(down_w[:, depths], two_frames(taps, 2 * chunk, depths), preferred_element_type=jnp.float32)

    pieces = [(run, chunk) for run in range(len(apart)) for chunk in range(chunks + 1)]
    waiting = []
    total = first_product(first_w, bands, pieces[0][0], apart[pieces[0][0]][1], pieces[0][1])
    for number, (run, chunk) in enumerate(pieces):
        beside = waiting.pop(0) if waiting else None
        parts = second_dot(*beside) if beside else None
        if number + 1 < len(pieces):
            later_run, later_chunk = pieces[number + 1]
            later = first_product(first_w, bands, later_run, apart[later_run][1], later_chunk)
        start, count = apart[run]
        activate(total, live_ref, range(start, start + count), chunk, act, held, 0, rows)
        if beside:
            second_rest(*beside, parts)
        total = later
        if chunk > 0:
            ready = [row for row in range(rows) if (row + 2 > rows) == (run > 0)]
            waiting += [(row, chunk - 1) for row in ready]
    for row, part in waiting:
        second_rest(row, part, second_dot(row, part))
    early = [down_conv(part, 0, rows) for part in range(chunks)]
    parts = [second_dot(rows, part) for part in range(chunks)]
    for part in range(chunks):
        second_rest(rows, part, parts[part])
    size = down_w.shape[0]
    for part in range(chunks):
        encoded = (early[part] + down_conv(part, rows, rows + 1)).astype(jnp.bfloat16)
        for t in range(2):
            frame = part * 2 + t
            out_ref[frame * size:(frame + 1) * size, :] = encoded[:, t * half:(t + 1) * half]


def hbm(array):
    return pltpu.with_memory_space_constraint(array, pltpu.HBM)


def snake(row_devices, frame_devices):
    route = []
    for left in range(0, frame_devices, 2):
        ring = [(row, left) for row in range(row_devices)] + [(row, left + 1) for row in reversed(range(row_devices))]
        ring = [row * frame_devices + frame for row, frame in ring]
        route += list(zip(ring, ring[1:] + ring[:1]))
    return route


def shards(pixels, frame_counts, weight_first, weight_second, weight_down):
    clips, frames, colors, rows, width = pixels.shape
    channels = weight_first.shape[3]
    half = width // 2
    out_rows = rows // 2
    frame_devices, row_devices = lax.axis_size("frames"), lax.axis_size("rows")
    assert clips == 1 and frames >= 4 and rows >= 3 and rows % 2 == 0 and frames % 2 == 0
    assert (GROUP + 2) * colors <= SLOT and frame_devices % 2 == 0
    bf16 = jnp.bfloat16
    frame_device = lax.axis_index("frames")
    size = frames * colors * rows
    earlier = lax.ppermute(pixels[0, -4:], "frames", [(i, (i + 1) % frame_devices) for i in range(frame_devices)])
    arrays = [
        hbm(pixels[0]),
        hbm(weight_first.transpose(0, 1, 2, 4, 3).reshape(TAPS**3, colors, channels)),
        hbm(weight_second.reshape(TAPS**3, channels, channels)),
        hbm(weight_down.reshape(TAPS**2, channels, channels)),
    ]
    loaded, weight_first, weight_second, weight_down = pl.pallas_call(
        load_kernel,
        name="load",
        compiler_params=pltpu.CompilerParams(vmem_limit_bytes=8 << 20),
        in_specs=[HBM] * len(arrays),
        out_specs=[VMEM] * len(arrays),
        out_shape=[jax.ShapeDtypeStruct(array.shape, bf16) for array in arrays],
        scratch_shapes=[pltpu.SemaphoreType.DMA((len(arrays),))],
    )(*arrays)
    late = loaded.reshape(size, width)
    earlier = earlier.reshape(4 * colors * rows, width)
    earlier = jnp.where(frame_device > 0, earlier, jnp.zeros_like(earlier))
    own = jnp.concatenate([earlier, late], axis=0)
    own, frame_counts = lax.optimization_barrier((own, frame_counts))
    route = snake(row_devices, frame_devices)
    axes = ("rows", "frames")
    back = lax.ppermute(own, axes, [(b, a) for a, b in route])
    there = lax.ppermute(own, axes, route)

    pair = PARITIES * channels
    wide = (frames + 2) * half
    depth = VIEWS * SLOT
    part = (frames + 4) // HALVES
    apart, alone = act_groups(rows)
    first_w, second_w, down_w, live, gather, columns, held_own, partial = pl.pallas_call(
        lambda *refs: prepare_kernel(*refs, rows=rows, frames=frames),
        name="prepare",
        compiler_params=pltpu.CompilerParams(vmem_limit_bytes=12 << 20),
        in_specs=[SMEM] + [VMEM] * 4,
        out_specs=[VMEM] * 8,
        out_shape=[
            jax.ShapeDtypeStruct((GROUP * pair, TAPS * depth), bf16),
            jax.ShapeDtypeStruct((pair, TAPS * TAPS * VIEWS * channels), bf16),
            jax.ShapeDtypeStruct((channels * out_rows, (rows + 1) * TAPS * channels), bf16),
            jax.ShapeDtypeStruct((rows + 3, wide), jnp.float32),
            jax.ShapeDtypeStruct((part * len(apart) * SLOT, 3 * own.shape[0] // HALVES), bf16),
            jax.ShapeDtypeStruct((width, VIEWS * half), bf16),
            jax.ShapeDtypeStruct((frames, (rows - 2) * pair, half), bf16),
            jax.ShapeDtypeStruct((rows, frames // 2, pair, 2 * half), jnp.float32),
        ],
        scratch_shapes=[
            pltpu.VMEM((frames + 4, len(alone) * depth, half), bf16),
            pltpu.VMEM((frames + 2, (rows - 2) * VIEWS * channels, half), bf16),
        ],
    )(frame_counts, own, weight_first, weight_second, weight_down)
    encoded = pl.pallas_call(
        lambda *refs: encode_kernel(*refs, rows=rows, frames=frames),
        name="encode",
        compiler_params=pltpu.CompilerParams(vmem_limit_bytes=24 << 20),
        in_specs=[VMEM] * 11,
        out_specs=VMEM,
        out_shape=jax.ShapeDtypeStruct((frames * channels * out_rows, half), bf16),
        scratch_shapes=[
            pltpu.VMEM((3 * own.shape[0], width), bf16),
            pltpu.VMEM((frames + 4, len(apart) * depth, half), bf16),
            pltpu.VMEM((frames + 2, (rows + 3) * VIEWS * channels, half), bf16),
            pltpu.VMEM((frames, (rows + 3) * pair, half), bf16),
            pltpu.VMEM((frames, (rows + 1) * TAPS * channels, half), bf16),
        ],
    )(own, there, back, gather, columns, live, held_own, partial, first_w, second_w, down_w)
    return encoded.reshape(1, frames, channels, out_rows, half)


def solution(mesh):
    in_specs = (
        P(("groups", "clips"), "frames", None, "rows", None),
        P(("groups", "clips")),
        P(),
        P(),
        P(),
    )
    out_specs = P(("groups", "clips"), "frames", None, "rows", None)
    return jax.shard_map(shards, mesh=mesh, in_specs=in_specs, out_specs=out_specs, check_vma=False)
```

time: 10.8 us -> 11.7 us (1.083)
  the two profiles are of different devices: /device:TPU:1 before, /device:TPU:0 now
where the time goes in v6:
time: 11.7 us; the launch traced here: 11.6 us
  Pallas kernels  6.05 us (52%)
  starting transfers between devices  3.32 us (28%)
  waiting for transfers between devices  1.46 us (12%)
  between operations  0.72 us (6%)
    pallas_call x1, Pallas kernels, shards(): pl.pallas_call(lambda *refs: encode_kernel(*refs, rows=rows, frames=frame...  2.98 us
    ppermute x1, starting transfers between devices, shards(): there = lax.ppermute(own, axes, route)  2.82 us
    pallas_call x1, Pallas kernels, shards(): pl.pallas_call(lambda *refs: prepare_kernel(*refs, rows=rows, frames=fram...  1.96 us
    ppermute x1, waiting for transfers between devices, shards(): back = lax.ppermute(own, axes, [(b, a) for a, b in route])  1.45 us
    pallas_call x1, Pallas kernels, shards(): pl.pallas_call(load_kernel, name='load', compiler_params=pltpu.CompilerPa...  1.11 us
    ppermute x1, starting transfers between devices, shards(): lax.ppermute(pixels[0, -4:], 'frames', [(i, (i + 1) % frame_devices) for...  0.49 us
  transfers between devices with their start and end apart: 3, of which 1 were waited for; matrix products, arithmetic and copies ran while one was open for 0% of the time, Pallas kernels for 27%

profile of v6, /device:TPU:0, one launch (start us, length us, event | category | flops | bytes accessed | tf_op | source)
XLA Modules:
  0.0 11.6 jit_solution(14327527190378474498)
XLA Ops:
  0.0 0.5 %collective-permute-start = (bf16[4,3,4,256]{3,2,1,0:T(4,128)(2,1)}, bf16[4,3,4,256]{3,2,1,0:T(4,128)(2,1)S(1)}, u32[]{:S(2)}, u32[]{:S(2)}) collective-permute-start(bf16[4,3,4,256]{3,2,1,0:T(4,128)(2,1)} %bitcast.10), channel_id=1, source_target_pairs={{0,1},{1,0},{2,3},{3,2},{4,5},{5,4},{6,7},{7,6},{8,9},{9,8},{10,11... | collective-permute-start | bytes 73736 | tf_op jit(solution)/shard_map/ppermute | solution.py:298
  0.5 1.1 %load.1 = (bf16[4,3,4,256]{3,2,1,0:T(4,128)(2,1)S(1)}, bf16[27,3,64]{2,1,0:T(4,128)(2,1)S(1)}, bf16[27,64,64]{2,1,0:T(8,128)(2,1)S(1)}, bf16[9,64,64]{2,1,0:T(8,128)(2,1)S(1)}) custom-call(bf16[4,3,4,256]{3,2,1,0:T(4,128)(2,1)} %bitcast.11, bf16[27,3,64]{2,1,0:T(4,128)(2,1)} %bitcast.9, bf16[27,64,64]{2,1,0:T(8,128)(2,1)} %bitcast.7, bf16[9,64,64]{2,1,0:T(8,128)(2,1)} %bitcast.8), custom_call_target="tpu_custom_call" | custom-call | tf_op jit(solution)/shard_map/load/pallas_call | solution.py:305
  1.6 0.0 collective-permute-done
  1.7 2.8 %collective-permute-start.1 = (bf16[96,256]{1,0:T(8,128)(2,1)S(1)}, bf16[96,256]{1,0:T(8,128)(2,1)S(1)}, u32[]{:S(2)}, u32[]{:S(2)}) collective-permute-start(bf16[96,256]{1,0:T(8,128)(2,1)S(1)} %pad_maximum_fusion.refs_1_.refs_0_), channel_id=1, source_target_pairs={{0,4},{4,8},{8,12},{12,13},{13,9},{9,5},{5,1},{1,0},{2,6},{6,10},{... | collective-permute-start | bytes 147464 | tf_op jit(solution)/shard_map/ppermute | solution.py:322
  4.5 0.0 collective-permute-start.2
  5.2 2.0 %prepare.1 = (bf16[384,192]{1,0:T(8,128)(2,1)S(1)}, bf16[128,2304]{1,0:T(8,128)(2,1)S(1)}, bf16[128,960]{1,0:T(8,128)(2,1)S(1)}, f32[7,768]{1,0:T(8,128)S(1)}, b...) custom-call(s32[1]{0:T(128)S(6)} %copy.6.refs_0_, ...), custom_call_target="tpu_custom_call" | custom-call | tf_op jit(solution)/shard_map/prepare/pallas_call | solution.py:329
  7.2 0.0 collective-permute-done.1.refs_1_
  7.2 1.5 %collective-permute-done.2.refs_2_ = bf16[96,256]{1,0:T(8,128)(2,1)S(1)} collective-permute-done((bf16[96,256]{1,0:T(8,128)(2,1)S(1)}, bf16[96,256]{1,0:T(8,128)(2,1)S(1)}, u32[]{:S(2)}, u32[]{:S(2)}) %collective-permute-start.2) | collective-permute-done | bytes 49184 | tf_op jit(solution)/shard_map/ppermute | solution.py:321
  8.6 3.0 %encode.1 = bf16[512,128]{1,0:T(8,128)(2,1)} custom-call(bf16[96,256]{1,0:T(8,128)(2,1)S(1)} %pad_maximum_fusion.refs_1_.refs_0_, bf16[96,256]{1,0:T(8,128)(2,1)S(1)} %collective-permute-done.1.refs_1_, bf16[96,256]{1,0:T(8,128)(2,1)S(1)} %collective-permute-done.2.refs_2_, bf16[128,144]{1,0:T(8,128)(2,1)S(1)} %get-tuple-element.25.refs_3_, ...), custom_call_target="tpu_custom_call" | custom-call | tf_op jit(solution)/shard_map/encode/pallas_call | solution.py:350
  (4 shorter events, 0.0 us)
Async XLA Ops:
  0.0 1.6 %collective-permute-start = (bf16[4,3,4,256]{3,2,1,0:T(4,128)(2,1)}, bf16[4,3,4,256]{3,2,1,0:T(4,128)(2,1)S(1)}, u32[]{:S(2)}, u32[]{:S(2)}) collective-permute-start(bf16[4,3,4,256]{3,2,1,0:T(4,128)(2,1)} %bitcast.10), channel_id=1, source_target_pairs={{0,1},{1,0},{2,3},{3,2},{4,5},{5,4},{6,7},{7,6},{8,9},{9,8},{10,11... | collective-permute-start | bytes 73736 | tf_op jit(solution)/shard_map/ppermute | solution.py:298
  1.7 5.4 %collective-permute-start.1 = (bf16[96,256]{1,0:T(8,128)(2,1)S(1)}, bf16[96,256]{1,0:T(8,128)(2,1)S(1)}, u32[]{:S(2)}, u32[]{:S(2)}) collective-permute-start(bf16[96,256]{1,0:T(8,128)(2,1)S(1)} %pad_maximum_fusion.refs_1_.refs_0_), channel_id=1, source_target_pairs={{0,4},{4,8},{8,12},{12,13},{13,9},{9,5},{5,1},{1,0},{2,6},{6,10},{... | collective-permute-start | bytes 147464 | tf_op jit(solution)/shard_map/ppermute | solution.py:322
  4.5 4.1 %collective-permute-start.2 = (bf16[96,256]{1,0:T(8,128)(2,1)S(1)}, bf16[96,256]{1,0:T(8,128)(2,1)S(1)}, u32[]{:S(2)}, u32[]{:S(2)}) collective-permute-start(bf16[96,256]{1,0:T(8,128)(2,1)S(1)} %pad_maximum_fusion.refs_1_.refs_0_), channel_id=1, source_target_pairs={{4,0},{8,4},{12,8},{13,12},{9,13},{5,9},{1,5},{0,1},{6,2},{10,6},{... | collective-permute-start | bytes 147464 | tf_op jit(solution)/shard_map/ppermute | solution.py:321

commit v7 on v6

--- a/solution.py
+++ b/solution.py
@@ -107,25 +107,20 @@
             act[frame, base + 3 * channels:base + 4 * channels, :] = to_left(value[:channels, inner])
 
 
-def load_kernel(*refs):
-    count = (len(refs) - 1) // 2
-    copies = [pltpu.make_async_copy(refs[i], refs[count + i], refs[-1].at[i]) for i in range(count)]
+def load_kernel(pixels_hbm, first_hbm, second_hbm, down_hbm, pixels, first, second, down, chosen, columns_out, gather_own, gather_out, sems, *, rows, frames):
+    arrays = ((pixels_hbm, pixels), (first_hbm, first), (second_hbm, second), (down_hbm, down))
+    copies = [pltpu.make_async_copy(source, target, sems.at[i]) for i, (source, target) in enumerate(arrays)]
     for copy in copies:
         copy.start()
-    for copy in copies:
-        copy.wait()
-
-
-def prepare_kernel(count, own, first, second, down, first_out, second_out, down_out, live_out, gather_out, columns_out, held_out, partial_out, bands, act, *, rows, frames):
-    channels = first.shape[2]
-    colors = first.shape[1]
+    colors = pixels.shape[1]
     apart, alone = act_groups(rows)
+    part = (frames + 4) // HALVES
 
     size = TAPS**3 * SUBLANES
     line = lax.broadcasted_iota(jnp.int32, (size, 1), 0)
     tap, color = line // SUBLANES, line % SUBLANES
     target = (tap // TAPS**2 * VIEWS + tap % TAPS) * SLOT + tap // TAPS % TAPS * colors + color
-    chosen = one_hot((size, first_out.shape[1]), target, color < colors)
+    chosen[...] = one_hot(chosen.shape, target, color < colors)
 
     width = columns_out.shape[0]
     column = lax.broadcasted_iota(jnp.int32, columns_out.shape, 0)
@@ -133,12 +128,36 @@
     half = width // 2
     columns_out[...] = jnp.where(column == place % half * 2 + place // half - 1, 1.0, 0.0).astype(jnp.bfloat16)
 
+    frame, color, row, used = band_targets(gather_own.shape[0], alone, colors)
+    gather_own[...] = one_hot(gather_own.shape, (frame * colors + color) * rows + row, used)
+
+    odd = lax.rem(lax.axis_index("frames"), 2)
+    frame, color, row, used = band_targets(gather_out.shape[0], apart, colors)
+    source = jnp.where(row < 0, 1 + odd, jnp.where(row < rows, 0, 2 - odd))
+    local = jnp.where(row < 0, row + rows, jnp.where(row < rows, row, row - rows))
+    gather_out[...] = one_hot(gather_out.shape, ((source * part + frame) * colors + color) * rows + local, used)
+
+    for copy in copies:
+        copy.wait()
+
+
+def prepare_kernel(count, own, first, second, down, chosen, columns, gather, first_out, second_out, down_out, live_out, held_out, partial_out, bands, act, *, rows, frames):
+    channels = first.shape[2]
+    colors = first.shape[1]
+    _, alone = act_groups(rows)
+    half = columns.shape[1] // VIEWS
+
+    none = jnp.zeros((channels, channels), jnp.bfloat16)
+    for tap in range(TAPS * TAPS):
+        taps = [second[tap * TAPS + tap_x] for tap_x in range(TAPS)]
+        depths = slice(tap * VIEWS * channels, (tap + 1) * VIEWS * channels)
+        second_out[:channels, depths] = jnp.concatenate(taps + [none], axis=1)
+        second_out[channels:, depths] = jnp.concatenate([none] + taps, axis=1)
+
     part = (frames + 4) // HALVES
     size = part * colors * rows
-    frame, color, row, used = band_targets(part * len(alone) * SLOT, alone, colors)
-    gather = one_hot((part * len(alone) * SLOT, size), (frame * colors + color) * rows + row, used)
     for number in range(HALVES):
-        spread_bands(gather, own[number * size:(number + 1) * size, :], columns_out[...], bands, number * part, alone)
+        spread_bands(gather[...], own[number * size:(number + 1) * size, :], columns[...], bands, number * part, alone)
 
     frame = lax.broadcasted_iota(jnp.int32, live_out.shape, 1) // half + (lax.axis_index("frames") * frames - 2)
     row = lax.broadcasted_iota(jnp.int32, live_out.shape, 0) + (lax.axis_index("rows") * rows - 2)
@@ -150,7 +169,7 @@
     for tap in range(TAPS**3):
         lines += [first[tap].astype(jnp.float32), filler]
     lines = jnp.concatenate(lines, axis=0).T.astype(jnp.bfloat16)
-    base = jnp.dot(lines, chosen, preferred_element_type=jnp.float32)
+    base = jnp.dot(lines, chosen[...], preferred_element_type=jnp.float32)
     for block in range(GROUP):
         for parity in range(PARITIES):
             shift = parity * SLOT + block * colors
@@ -162,19 +181,6 @@
         for chunk in range(frames // 2 + 1):
             total = first_product(first_out, bands, run, rows_of, chunk)
             activate(total, live_out, range(start, start + rows_of), chunk, act, held_out, 3, rows)
-
-    odd = lax.rem(lax.axis_index("frames"), 2)
-    frame, color, row, used = band_targets(gather_out.shape[0], apart, colors)
-    source = jnp.where(row < 0, 1 + odd, jnp.where(row < rows, 0, 2 - odd))
-    local = jnp.where(row < 0, row + rows, jnp.where(row < rows, row, row - rows))
-    gather_out[...] = one_hot(gather_out.shape, ((source * part + frame) * colors + color) * rows + local, used)
-
-    none = jnp.zeros((channels, channels), jnp.bfloat16)
-    for tap in range(TAPS * TAPS):
-        taps = [second[tap * TAPS + tap_x] for tap_x in range(TAPS)]
-        columns = slice(tap * VIEWS * channels, (tap + 1) * VIEWS * channels)
-        second_out[:channels, columns] = jnp.concatenate(taps + [none], axis=1)
-        second_out[channels:, columns] = jnp.concatenate([none] + taps, axis=1)
 
     for row in range(1, rows + 1):
         for chunk in range(frames // 2):
@@ -302,13 +308,22 @@
         hbm(weight_second.reshape(TAPS**3, channels, channels)),
         hbm(weight_down.reshape(TAPS**2, channels, channels)),
     ]
-    loaded, weight_first, weight_second, weight_down = pl.pallas_call(
-        load_kernel,
+    apart, alone = act_groups(rows)
+    part = (frames + 4) // HALVES
+    lines = part * colors * rows
+    shapes = [array.shape for array in arrays] + [
+        (TAPS**3 * SUBLANES, TAPS * VIEWS * SLOT),
+        (width, VIEWS * half),
+        (part * len(alone) * SLOT, lines),
+        (part * len(apart) * SLOT, 3 * lines),
+    ]
+    loaded, weight_first, weight_second, weight_down, chosen, columns, gather_own, gather = pl.pallas_call(
+        lambda *refs: load_kernel(*refs, rows=rows, frames=frames),
         name="load",
         compiler_params=pltpu.CompilerParams(vmem_limit_bytes=8 << 20),
         in_specs=[HBM] * len(arrays),
-        out_specs=[VMEM] * len(arrays),
-        out_shape=[jax.ShapeDtypeStruct(array.shape, bf16) for array in arrays],
+        out_specs=[VMEM] * len(shapes),
+        out_shape=[jax.ShapeDtypeStruct(shape, bf16) for shape in shapes],
         scratch_shapes=[pltpu.SemaphoreType.DMA((len(arrays),))],
     )(*arrays)
     late = loaded.reshape(size, width)
@@ -324,21 +339,17 @@
     pair = PARITIES * channels
     wide = (frames + 2) * half
     depth = VIEWS * SLOT
-    part = (frames + 4) // HALVES
-    apart, alone = act_groups(rows)
-    first_w, second_w, down_w, live, gather, columns, held_own, partial = pl.pallas_call(
+    first_w, second_w, down_w, live, held_own, partial = pl.pallas_call(
         lambda *refs: prepare_kernel(*refs, rows=rows, frames=frames),
         name="prepare",
         compiler_params=pltpu.CompilerParams(vmem_limit_bytes=12 << 20),
-        in_specs=[SMEM] + [VMEM] * 4,
-        out_specs=[VMEM] * 8,
+        in_specs=[SMEM] + [VMEM] * 7,
+        out_specs=[VMEM] * 6,
         out_shape=[
             jax.ShapeDtypeStruct((GROUP * pair, TAPS * depth), bf16),
             jax.ShapeDtypeStruct((pair, TAPS * TAPS * VIEWS * channels), bf16),
             jax.ShapeDtypeStruct((channels * out_rows, (rows + 1) * TAPS * channels), bf16),
             jax.ShapeDtypeStruct((rows + 3, wide), jnp.float32),
-            jax.ShapeDtypeStruct((part * len(apart) * SLOT, 3 * own.shape[0] // HALVES), bf16),
-            jax.ShapeDtypeStruct((width, VIEWS * half), bf16),
             jax.ShapeDtypeStruct((frames, (rows - 2) * pair, half), bf16),
             jax.ShapeDtypeStruct((rows, frames // 2, pair, 2 * half), jnp.float32),
         ],
@@ -346,7 +357,7 @@
             pltpu.VMEM((frames + 4, len(alone) * depth, half), bf16),
             pltpu.VMEM((frames + 2, (rows - 2) * VIEWS * channels, half), bf16),
         ],
-    )(frame_counts, own, weight_first, weight_second, weight_down)
+    )(frame_counts, own, weight_first, weight_second, weight_down, chosen, columns, gather_own)
     encoded = pl.pallas_call(
         lambda *refs: encode_kernel(*refs, rows=rows, frames=frames),
         name="encode",

time: 11.7 us -> 11.7 us (level)
  transfers between devices with their start and end apart: 3 -> 3, of which waited for: 1 -> 1; matrix products, arithmetic and copies ran while one was open for 0% -> 0% of each run, Pallas kernels for 27% -> 26%
where the time goes in v7:
time: 11.7 us; the launch traced here: 11.6 us
  Pallas kernels  5.94 us (51%)
  starting transfers between devices  3.32 us (28%)
  waiting for transfers between devices  1.57 us (13%)
  between operations  0.72 us (6%)
    pallas_call x1, Pallas kernels, shards(): pl.pallas_call(lambda *refs: encode_kernel(*refs, rows=rows, frames=frame...  2.98 us
    ppermute x1, starting transfers between devices, shards(): there = lax.ppermute(own, axes, route)  2.82 us
    pallas_call x1, Pallas kernels, shards(): pl.pallas_call(lambda *refs: prepare_kernel(*refs, rows=rows, frames=fram...  1.85 us
    ppermute x1, waiting for transfers between devices, shards(): back = lax.ppermute(own, axes, [(b, a) for a, b in route])  1.57 us
    pallas_call x1, Pallas kernels, shards(): pl.pallas_call(lambda *refs: load_kernel(*refs, rows=rows, frames=frames)...  1.11 us
    ppermute x1, starting transfers between devices, shards(): lax.ppermute(pixels[0, -4:], 'frames', [(i, (i + 1) % frame_devices) for...  0.49 us
  transfers between devices with their start and end apart: 3, of which 1 were waited for; matrix products, arithmetic and copies ran while one was open for 0% of the time, Pallas kernels for 26%

profile of v7, /device:TPU:0, one launch (start us, length us, event | category | flops | bytes accessed | tf_op | source)
XLA Modules:
  0.0 11.6 jit_solution(15713107663555589213)
XLA Ops:
  0.0 0.5 %collective-permute-start = (bf16[4,3,4,256]{3,2,1,0:T(4,128)(2,1)}, bf16[4,3,4,256]{3,2,1,0:T(4,128)(2,1)S(1)}, u32[]{:S(2)}, u32[]{:S(2)}) collective-permute-start(bf16[4,3,4,256]{3,2,1,0:T(4,128)(2,1)} %bitcast.10), channel_id=1, source_target_pairs={{0,1},{1,0},{2,3},{3,2},{4,5},{5,4},{6,7},{7,6},{8,9},{9,8},{10,11... | collective-permute-start | bytes 73736 | tf_op jit(solution)/shard_map/ppermute | solution.py:304
  0.5 1.1 %load.1 = (bf16[4,3,4,256]{3,2,1,0:T(4,128)(2,1)S(1)}, bf16[27,3,64]{2,1,0:T(4,128)(2,1)S(1)}, bf16[27,64,64]{2,1,0:T(8,128)(2,1)S(1)}, bf16[9,64,64]{2,1,0:T(8,...) custom-call(bf16[4,3,4,256]{3,2,1,0:T(4,128)(2,1)} %bitcast.11, ...), custom_call_target="tpu_custom_call" | custom-call | tf_op jit(solution)/shard_map/load/pallas_call | solution.py:320
  1.6 0.0 collective-permute-done
  1.7 2.8 %collective-permute-start.1 = (bf16[96,256]{1,0:T(8,128)(2,1)S(1)}, bf16[96,256]{1,0:T(8,128)(2,1)S(1)}, u32[]{:S(2)}, u32[]{:S(2)}) collective-permute-start(bf16[96,256]{1,0:T(8,128)(2,1)S(1)} %pad_maximum_fusion.refs_1_.refs_0_), channel_id=1, source_target_pairs={{0,4},{4,8},{8,12},{12,13},{13,9},{9,5},{5,1},{1,0},{2,6},{6,10},{... | collective-permute-start | bytes 147464 | tf_op jit(solution)/shard_map/ppermute | solution.py:337
  4.5 0.0 collective-permute-start.2
  5.2 1.8 %prepare.1 = (bf16[384,192]{1,0:T(8,128)(2,1)S(1)}, bf16[128,2304]{1,0:T(8,128)(2,1)S(1)}, bf16[128,960]{1,0:T(8,128)(2,1)S(1)}, f32[7,768]{1,0:T(8,128)S(1)}, b...) custom-call(s32[1]{0:T(128)S(6)} %copy.6.refs_0_, bf16[96,256]{1,0:T(8,128)(2,1)S(1)} %pad_maximum_fusion.refs_1_.refs_0_, ...), custom_call_target="tpu_custom_call" | custom-call | tf_op jit(solution)/shard_map/prepare/pallas_call | solution.py:342
  7.0 0.0 collective-permute-done.1.refs_1_
  7.0 1.6 %collective-permute-done.2.refs_2_ = bf16[96,256]{1,0:T(8,128)(2,1)S(1)} collective-permute-done((bf16[96,256]{1,0:T(8,128)(2,1)S(1)}, bf16[96,256]{1,0:T(8,128)(2,1)S(1)}, u32[]{:S(2)}, u32[]{:S(2)}) %collective-permute-start.2) | collective-permute-done | bytes 49184 | tf_op jit(solution)/shard_map/ppermute | solution.py:336
  8.6 3.0 %encode.1 = bf16[512,128]{1,0:T(8,128)(2,1)} custom-call(bf16[96,256]{1,0:T(8,128)(2,1)S(1)} %pad_maximum_fusion.refs_1_.refs_0_, bf16[96,256]{1,0:T(8,128)(2,1)S(1)} %collective-permute-done.1.refs_1_, bf16[96,256]{1,0:T(8,128)(2,1)S(1)} %collective-permute-done.2.refs_2_, bf16[128,144]{1,0:T(8,128)(2,1)S(1)} %get-tuple-element.23.refs_3_, ...), custom_call_target="tpu_custom_call" | custom-call | tf_op jit(solution)/shard_map/encode/pallas_call | solution.py:361
  (4 shorter events, 0.0 us)
Async XLA Ops:
  0.0 1.6 %collective-permute-start = (bf16[4,3,4,256]{3,2,1,0:T(4,128)(2,1)}, bf16[4,3,4,256]{3,2,1,0:T(4,128)(2,1)S(1)}, u32[]{:S(2)}, u32[]{:S(2)}) collective-permute-start(bf16[4,3,4,256]{3,2,1,0:T(4,128)(2,1)} %bitcast.10), channel_id=1, source_target_pairs={{0,1},{1,0},{2,3},{3,2},{4,5},{5,4},{6,7},{7,6},{8,9},{9,8},{10,11... | collective-permute-start | bytes 73736 | tf_op jit(solution)/shard_map/ppermute | solution.py:304
  1.7 5.3 %collective-permute-start.1 = (bf16[96,256]{1,0:T(8,128)(2,1)S(1)}, bf16[96,256]{1,0:T(8,128)(2,1)S(1)}, u32[]{:S(2)}, u32[]{:S(2)}) collective-permute-start(bf16[96,256]{1,0:T(8,128)(2,1)S(1)} %pad_maximum_fusion.refs_1_.refs_0_), channel_id=1, source_target_pairs={{0,4},{4,8},{8,12},{12,13},{13,9},{9,5},{5,1},{1,0},{2,6},{6,10},{... | collective-permute-start | bytes 147464 | tf_op jit(solution)/shard_map/ppermute | solution.py:337
  4.5 4.1 %collective-permute-start.2 = (bf16[96,256]{1,0:T(8,128)(2,1)S(1)}, bf16[96,256]{1,0:T(8,128)(2,1)S(1)}, u32[]{:S(2)}, u32[]{:S(2)}) collective-permute-start(bf16[96,256]{1,0:T(8,128)(2,1)S(1)} %pad_maximum_fusion.refs_1_.refs_0_), channel_id=1, source_target_pairs={{4,0},{8,4},{12,8},{13,12},{9,13},{5,9},{1,5},{0,1},{6,2},{10,6},{... | collective-permute-start | bytes 147464 | tf_op jit(solution)/shard_map/ppermute | solution.py:336

commit v8 on v7

--- a/solution.py
+++ b/solution.py
@@ -182,10 +182,6 @@
             total = first_product(first_out, bands, run, rows_of, chunk)
             activate(total, live_out, range(start, start + rows_of), chunk, act, held_out, 3, rows)
 
-    for row in range(1, rows + 1):
-        for chunk in range(frames // 2):
-            partial_out[row - 1, chunk] = second_product(second_out, lambda line: (act, line - 3), row, chunk, tap_rows(row, rows, True))
-
     out_rows = down_out.shape[0] // channels
     sum_rows = down_out.shape[1] // (TAPS * channels)
     taps = jnp.concatenate([down[tap] for tap in range(TAPS * TAPS)], axis=1)
@@ -203,6 +199,10 @@
         part = jnp.dot(spread, jnp.concatenate(pieces, axis=1), preferred_element_type=jnp.float32)
         total = part if total is None else total + part
     down_out[...] = total.astype(jnp.bfloat16)
+
+    for row in range(1, rows + 1):
+        for chunk in range(frames // 2):
+            partial_out[row - 1, chunk] = second_product(second_out, lambda line: (act, line - 3), row, chunk, tap_rows(row, rows, True))
 
 
 def encode_kernel(own_ref, there_ref, back_ref, gather_ref, columns_ref, live_ref, held_own, partial_ref, first_w, second_w, down_w, out_ref, lines, bands, act, held, taps, *, rows, frames):
@@ -263,10 +263,13 @@
         if chunk > 0:
             ready = [row for row in range(rows) if (row + 2 > rows) == (run > 0)]
             waiting += [(row, chunk - 1) for row in ready]
+    early = None
     for row, part in waiting:
+        if row == rows - 1 and early is None:
+            early = [down_conv(chunk, 0, rows - 2) for chunk in range(chunks)]
         second_rest(row, part, second_dot(row, part))
-    early = [down_conv(part, 0, rows) for part in range(chunks)]
     parts = [second_dot(rows, part) for part in range(chunks)]
+    early = [early[chunk] + down_conv(chunk, rows - 2, rows) for chunk in range(chunks)]
     for part in range(chunks):
         second_rest(rows, part, parts[part])
     size = down_w.shape[0]

time: 11.7 us -> 11.6 us (level)
  Pallas kernels: 5.94 us -> 5.72 us
  waiting for transfers between devices: 1.57 us -> 1.69 us
  transfers between devices with their start and end apart: 3 -> 3, of which waited for: 1 -> 1; matrix products, arithmetic and copies ran while one was open for 0% -> 0% of each run, Pallas kernels for 26% -> 25%
where the time goes in v8:
time: 11.6 us; the launch traced here: 11.5 us
  Pallas kernels  5.72 us (49%)
  starting transfers between devices  3.32 us (29%)
  waiting for transfers between devices  1.69 us (15%)
  between operations  0.72 us (6%)
    pallas_call x1, Pallas kernels, shards(): pl.pallas_call(lambda *refs: encode_kernel(*refs, rows=rows, frames=frame...  2.87 us
    ppermute x1, starting transfers between devices, shards(): there = lax.ppermute(own, axes, route)  2.82 us
    pallas_call x1, Pallas kernels, shards(): pl.pallas_call(lambda *refs: prepare_kernel(*refs, rows=rows, frames=fram...  1.74 us
    ppermute x1, waiting for transfers between devices, shards(): back = lax.ppermute(own, axes, [(b, a) for a, b in route])  1.68 us
    pallas_call x1, Pallas kernels, shards(): pl.pallas_call(lambda *refs: load_kernel(*refs, rows=rows, frames=frames)...  1.11 us
    ppermute x1, starting transfers between devices, shards(): lax.ppermute(pixels[0, -4:], 'frames', [(i, (i + 1) % frame_devices) for...  0.49 us
  transfers between devices with their start and end apart: 3, of which 1 were waited for; matrix products, arithmetic and copies ran while one was open for 0% of the time, Pallas kernels for 25%

profile of v8, /device:TPU:0, one launch (start us, length us, event | category | flops | bytes accessed | tf_op | source)
XLA Modules:
  0.0 11.5 jit_solution(9302919061679296164)
XLA Ops:
  0.0 0.5 %collective-permute-start = (bf16[4,3,4,256]{3,2,1,0:T(4,128)(2,1)}, bf16[4,3,4,256]{3,2,1,0:T(4,128)(2,1)S(1)}, u32[]{:S(2)}, u32[]{:S(2)}) collective-permute-start(bf16[4,3,4,256]{3,2,1,0:T(4,128)(2,1)} %bitcast.10), channel_id=1, source_target_pairs={{0,1},{1,0},{2,3},{3,2},{4,5},{5,4},{6,7},{7,6},{8,9},{9,8},{10,11... | collective-permute-start | bytes 73736 | tf_op jit(solution)/shard_map/ppermute | solution.py:307
  0.5 1.1 %load.1 = (bf16[4,3,4,256]{3,2,1,0:T(4,128)(2,1)S(1)}, bf16[27,3,64]{2,1,0:T(4,128)(2,1)S(1)}, bf16[27,64,64]{2,1,0:T(8,128)(2,1)S(1)}, bf16[9,64,64]{2,1,0:T(8,...) custom-call(bf16[4,3,4,256]{3,2,1,0:T(4,128)(2,1)} %bitcast.11, ...), custom_call_target="tpu_custom_call" | custom-call | tf_op jit(solution)/shard_map/load/pallas_call | solution.py:323
  1.6 0.0 collective-permute-done
  1.7 2.8 %collective-permute-start.1 = (bf16[96,256]{1,0:T(8,128)(2,1)S(1)}, bf16[96,256]{1,0:T(8,128)(2,1)S(1)}, u32[]{:S(2)}, u32[]{:S(2)}) collective-permute-start(bf16[96,256]{1,0:T(8,128)(2,1)S(1)} %pad_maximum_fusion.refs_1_.refs_0_), channel_id=1, source_target_pairs={{0,4},{4,8},{8,12},{12,13},{13,9},{9,5},{5,1},{1,0},{2,6},{6,10},{... | collective-permute-start | bytes 147464 | tf_op jit(solution)/shard_map/ppermute | solution.py:340
  4.5 0.0 collective-permute-start.2
  5.2 1.7 %prepare.1 = (bf16[384,192]{1,0:T(8,128)(2,1)S(1)}, bf16[128,2304]{1,0:T(8,128)(2,1)S(1)}, bf16[128,960]{1,0:T(8,128)(2,1)S(1)}, f32[7,768]{1,0:T(8,128)S(1)}, b...) custom-call(s32[1]{0:T(128)S(6)} %copy.6.refs_0_, bf16[96,256]{1,0:T(8,128)(2,1)S(1)} %pad_maximum_fusion.refs_1_.refs_0_, ...), custom_call_target="tpu_custom_call" | custom-call | tf_op jit(solution)/shard_map/prepare/pallas_call | solution.py:345
  6.9 0.0 collective-permute-done.1.refs_1_
  6.9 1.7 %collective-permute-done.2.refs_2_ = bf16[96,256]{1,0:T(8,128)(2,1)S(1)} collective-permute-done((bf16[96,256]{1,0:T(8,128)(2,1)S(1)}, bf16[96,256]{1,0:T(8,128)(2,1)S(1)}, u32[]{:S(2)}, u32[]{:S(2)}) %collective-permute-start.2) | collective-permute-done | bytes 49184 | tf_op jit(solution)/shard_map/ppermute | solution.py:339
  8.6 2.9 %encode.1 = bf16[512,128]{1,0:T(8,128)(2,1)} custom-call(bf16[96,256]{1,0:T(8,128)(2,1)S(1)} %pad_maximum_fusion.refs_1_.refs_0_, bf16[96,256]{1,0:T(8,128)(2,1)S(1)} %collective-permute-done.1.refs_1_, bf16[96,256]{1,0:T(8,128)(2,1)S(1)} %collective-permute-done.2.refs_2_, bf16[128,144]{1,0:T(8,128)(2,1)S(1)} %get-tuple-element.23.refs_3_, ...), custom_call_target="tpu_custom_call" | custom-call | tf_op jit(solution)/shard_map/encode/pallas_call | solution.py:364
  (4 shorter events, 0.0 us)
Async XLA Ops:
  0.0 1.6 %collective-permute-start = (bf16[4,3,4,256]{3,2,1,0:T(4,128)(2,1)}, bf16[4,3,4,256]{3,2,1,0:T(4,128)(2,1)S(1)}, u32[]{:S(2)}, u32[]{:S(2)}) collective-permute-start(bf16[4,3,4,256]{3,2,1,0:T(4,128)(2,1)} %bitcast.10), channel_id=1, source_target_pairs={{0,1},{1,0},{2,3},{3,2},{4,5},{5,4},{6,7},{7,6},{8,9},{9,8},{10,11... | collective-permute-start | bytes 73736 | tf_op jit(solution)/shard_map/ppermute | solution.py:307
  1.7 5.2 %collective-permute-start.1 = (bf16[96,256]{1,0:T(8,128)(2,1)S(1)}, bf16[96,256]{1,0:T(8,128)(2,1)S(1)}, u32[]{:S(2)}, u32[]{:S(2)}) collective-permute-start(bf16[96,256]{1,0:T(8,128)(2,1)S(1)} %pad_maximum_fusion.refs_1_.refs_0_), channel_id=1, source_target_pairs={{0,4},{4,8},{8,12},{12,13},{13,9},{9,5},{5,1},{1,0},{2,6},{6,10},{... | collective-permute-start | bytes 147464 | tf_op jit(solution)/shard_map/ppermute | solution.py:340
  4.5 4.1 %collective-permute-start.2 = (bf16[96,256]{1,0:T(8,128)(2,1)S(1)}, bf16[96,256]{1,0:T(8,128)(2,1)S(1)}, u32[]{:S(2)}, u32[]{:S(2)}) collective-permute-start(bf16[96,256]{1,0:T(8,128)(2,1)S(1)} %pad_maximum_fusion.refs_1_.refs_0_), channel_id=1, source_target_pairs={{4,0},{8,4},{12,8},{13,12},{9,13},{5,9},{1,5},{0,1},{6,2},{10,6},{... | collective-permute-start | bytes 147464 | tf_op jit(solution)/shard_map/ppermute | solution.py:339

commit v9 on v8

--- a/solution.py
+++ b/solution.py
@@ -94,7 +94,7 @@
     for block, row in enumerate(rows_of):
         mask = live[row:row + 1, 2 * chunk * half:2 * (chunk + 1) * half].astype(jnp.bfloat16)
         first = total[block * pair:(block + 1) * pair, :].astype(jnp.bfloat16) * mask
-        value = 0.5 * first.astype(jnp.float32)
+        value = first.astype(jnp.float32)
         value = (value + value * jnp.tanh(value)).astype(jnp.bfloat16)
         base = (row - base_row) * VIEWS * channels
         for t in range(2):
@@ -169,7 +169,7 @@
     for tap in range(TAPS**3):
         lines += [first[tap].astype(jnp.float32), filler]
     lines = jnp.concatenate(lines, axis=0).T.astype(jnp.bfloat16)
-    base = jnp.dot(lines, chosen[...], preferred_element_type=jnp.float32)
+    base = 0.5 * jnp.dot(lines, chosen[...], preferred_element_type=jnp.float32)
     for block in range(GROUP):
         for parity in range(PARITIES):
             shift = parity * SLOT + block * colors
@@ -235,7 +235,7 @@
         second = total * live_ref[row + 1:row + 2, (chunk + 1) * step:(chunk + 2) * step]
         source, base = (held_own, row - 2) if 3 <= row + 1 <= rows else (held, row + 1)
         first = two_frames(source, 2 * chunk, slice(base * pair, (base + 1) * pair))
-        value = (first.astype(jnp.float32) + second).astype(jnp.bfloat16)
+        value = (2 * first.astype(jnp.float32) + second).astype(jnp.bfloat16)
         base = row * TAPS * channels
         for t in range(2):
             inner = slice(t * half, (t + 1) * half)

time: 11.6 us -> 11.6 us (level)
  no operation moved by 1% of the time
where the time goes in v9:
time: 11.6 us; the launch traced here: 11.5 us
  Pallas kernels  5.72 us (49%)
  starting transfers between devices  3.32 us (29%)
  waiting for transfers between devices  1.69 us (15%)
  between operations  0.72 us (6%)
    pallas_call x1, Pallas kernels, shards(): pl.pallas_call(lambda *refs: encode_kernel(*refs, rows=rows, frames=frame...  2.87 us
    ppermute x1, starting transfers between devices, shards(): there = lax.ppermute(own, axes, route)  2.82 us
    pallas_call x1, Pallas kernels, shards(): pl.pallas_call(lambda *refs: prepare_kernel(*refs, rows=rows, frames=fram...  1.73 us
    ppermute x1, waiting for transfers between devices, shards(): back = lax.ppermute(own, axes, [(b, a) for a, b in route])  1.69 us
    pallas_call x1, Pallas kernels, shards(): pl.pallas_call(lambda *refs: load_kernel(*refs, rows=rows, frames=frames)...  1.11 us
    ppermute x1, starting transfers between devices, shards(): lax.ppermute(pixels[0, -4:], 'frames', [(i, (i + 1) % frame_devices) for...  0.49 us
  transfers between devices with their start and end apart: 3, of which 1 were waited for; matrix products, arithmetic and copies ran while one was open for 0% of the time, Pallas kernels for 25%

profile of v9, /device:TPU:0, one launch (start us, length us, event | category | flops | bytes accessed | tf_op | source)
XLA Modules:
  0.0 11.5 jit_solution(9205534323711030149)
XLA Ops:
  0.0 0.5 %collective-permute-start = (bf16[4,3,4,256]{3,2,1,0:T(4,128)(2,1)}, bf16[4,3,4,256]{3,2,1,0:T(4,128)(2,1)S(1)}, u32[]{:S(2)}, u32[]{:S(2)}) collective-permute-start(bf16[4,3,4,256]{3,2,1,0:T(4,128)(2,1)} %bitcast.10), channel_id=1, source_target_pairs={{0,1},{1,0},{2,3},{3,2},{4,5},{5,4},{6,7},{7,6},{8,9},{9,8},{10,11... | collective-permute-start | bytes 73736 | tf_op jit(solution)/shard_map/ppermute | solution.py:307
  0.5 1.1 %load.1 = (bf16[4,3,4,256]{3,2,1,0:T(4,128)(2,1)S(1)}, bf16[27,3,64]{2,1,0:T(4,128)(2,1)S(1)}, bf16[27,64,64]{2,1,0:T(8,128)(2,1)S(1)}, bf16[9,64,64]{2,1,0:T(8,...) custom-call(bf16[4,3,4,256]{3,2,1,0:T(4,128)(2,1)} %bitcast.11, ...), custom_call_target="tpu_custom_call" | custom-call | tf_op jit(solution)/shard_map/load/pallas_call | solution.py:323
  1.6 0.0 collective-permute-done
  1.7 2.8 %collective-permute-start.1 = (bf16[96,256]{1,0:T(8,128)(2,1)S(1)}, bf16[96,256]{1,0:T(8,128)(2,1)S(1)}, u32[]{:S(2)}, u32[]{:S(2)}) collective-permute-start(bf16[96,256]{1,0:T(8,128)(2,1)S(1)} %pad_maximum_fusion.refs_1_.refs_0_), channel_id=1, source_target_pairs={{0,4},{4,8},{8,12},{12,13},{13,9},{9,5},{5,1},{1,0},{2,6},{6,10},{... | collective-permute-start | bytes 147464 | tf_op jit(solution)/shard_map/ppermute | solution.py:340
  4.5 0.0 collective-permute-start.2
  5.2 1.7 %prepare.1 = (bf16[384,192]{1,0:T(8,128)(2,1)S(1)}, bf16[128,2304]{1,0:T(8,128)(2,1)S(1)}, bf16[128,960]{1,0:T(8,128)(2,1)S(1)}, f32[7,768]{1,0:T(8,128)S(1)}, b...) custom-call(s32[1]{0:T(128)S(6)} %copy.6.refs_0_, bf16[96,256]{1,0:T(8,128)(2,1)S(1)} %pad_maximum_fusion.refs_1_.refs_0_, ...), custom_call_target="tpu_custom_call" | custom-call | tf_op jit(solution)/shard_map/prepare/pallas_call | solution.py:345
  6.9 0.0 collective-permute-done.1.refs_1_
  6.9 1.7 %collective-permute-done.2.refs_2_ = bf16[96,256]{1,0:T(8,128)(2,1)S(1)} collective-permute-done((bf16[96,256]{1,0:T(8,128)(2,1)S(1)}, bf16[96,256]{1,0:T(8,128)(2,1)S(1)}, u32[]{:S(2)}, u32[]{:S(2)}) %collective-permute-start.2) | collective-permute-done | bytes 49184 | tf_op jit(solution)/shard_map/ppermute | solution.py:339
  8.6 2.9 %encode.1 = bf16[512,128]{1,0:T(8,128)(2,1)} custom-call(bf16[96,256]{1,0:T(8,128)(2,1)S(1)} %pad_maximum_fusion.refs_1_.refs_0_, bf16[96,256]{1,0:T(8,128)(2,1)S(1)} %collective-permute-done.1.refs_1_, bf16[96,256]{1,0:T(8,128)(2,1)S(1)} %collective-permute-done.2.refs_2_, bf16[128,144]{1,0:T(8,128)(2,1)S(1)} %get-tuple-element.23.refs_3_, ...), custom_call_target="tpu_custom_call" | custom-call | tf_op jit(solution)/shard_map/encode/pallas_call | solution.py:364
  (4 shorter events, 0.0 us)
Async XLA Ops:
  0.0 1.6 %collective-permute-start = (bf16[4,3,4,256]{3,2,1,0:T(4,128)(2,1)}, bf16[4,3,4,256]{3,2,1,0:T(4,128)(2,1)S(1)}, u32[]{:S(2)}, u32[]{:S(2)}) collective-permute-start(bf16[4,3,4,256]{3,2,1,0:T(4,128)(2,1)} %bitcast.10), channel_id=1, source_target_pairs={{0,1},{1,0},{2,3},{3,2},{4,5},{5,4},{6,7},{7,6},{8,9},{9,8},{10,11... | collective-permute-start | bytes 73736 | tf_op jit(solution)/shard_map/ppermute | solution.py:307
  1.7 5.2 %collective-permute-start.1 = (bf16[96,256]{1,0:T(8,128)(2,1)S(1)}, bf16[96,256]{1,0:T(8,128)(2,1)S(1)}, u32[]{:S(2)}, u32[]{:S(2)}) collective-permute-start(bf16[96,256]{1,0:T(8,128)(2,1)S(1)} %pad_maximum_fusion.refs_1_.refs_0_), channel_id=1, source_target_pairs={{0,4},{4,8},{8,12},{12,13},{13,9},{9,5},{5,1},{1,0},{2,6},{6,10},{... | collective-permute-start | bytes 147464 | tf_op jit(solution)/shard_map/ppermute | solution.py:340
  4.5 4.1 %collective-permute-start.2 = (bf16[96,256]{1,0:T(8,128)(2,1)S(1)}, bf16[96,256]{1,0:T(8,128)(2,1)S(1)}, u32[]{:S(2)}, u32[]{:S(2)}) collective-permute-start(bf16[96,256]{1,0:T(8,128)(2,1)S(1)} %pad_maximum_fusion.refs_1_.refs_0_), channel_id=1, source_target_pairs={{4,0},{8,4},{12,8},{13,12},{9,13},{5,9},{1,5},{0,1},{6,2},{10,6},{... | collective-permute-start | bytes 147464 | tf_op jit(solution)/shard_map/ppermute | solution.py:339

commit v10 on v8

--- a/solution.py
+++ b/solution.py
@@ -178,8 +178,8 @@
             first_out[start:start + channels, :] = moved.astype(jnp.bfloat16)
 
     for run, (start, rows_of) in enumerate(alone):
-        for chunk in range(frames // 2 + 1):
-            total = first_product(first_out, bands, run, rows_of, chunk)
+        totals = [first_product(first_out, bands, run, rows_of, chunk) for chunk in range(frames // 2 + 1)]
+        for chunk, total in enumerate(totals):
             activate(total, live_out, range(start, start + rows_of), chunk, act, held_out, 3, rows)
 
     out_rows = down_out.shape[0] // channels
@@ -205,7 +205,7 @@
             partial_out[row - 1, chunk] = second_product(second_out, lambda line: (act, line - 3), row, chunk, tap_rows(row, rows, True))
 
 
-def encode_kernel(own_ref, there_ref, back_ref, gather_ref, columns_ref, live_ref, held_own, partial_ref, first_w, second_w, down_w, out_ref, lines, bands, act, held, taps, *, rows, frames):
+def encode_kernel(own_ref, there_ref, back_ref, gather_ref, columns_ref, live_ref, held_own, partial_ref, first_w, second_w, down_w, out_ref, bands, act, held, taps, *, rows, frames):
     half = columns_ref.shape[1] // VIEWS
     channels = second_w.shape[0] // PARITIES
     pair = PARITIES * channels
@@ -218,11 +218,8 @@
     size = own_ref.shape[0] // HALVES
     for part in range(HALVES):
         rows_of = slice(part * size, (part + 1) * size)
-        base = part * 3 * size
-        lines[base:base + size, :] = own_ref[rows_of, :]
-        lines[base + size:base + 2 * size, :] = there_ref[rows_of, :] * keep_there
-        lines[base + 2 * size:base + 3 * size, :] = back_ref[rows_of, :] * keep_back
-        spread_bands(gather_ref[...], lines[base:base + 3 * size, :], columns_ref[...], bands, part * (frames + 4) // HALVES, apart)
+        lines = jnp.concatenate([own_ref[rows_of, :], there_ref[rows_of, :] * keep_there, back_ref[rows_of, :] * keep_back], axis=0)
+        spread_bands(gather_ref[...], lines, columns_ref[...], bands, part * (frames + 4) // HALVES, apart)
 
     step = 2 * half
     chunks = frames // 2
@@ -369,7 +366,6 @@
         out_specs=VMEM,
         out_shape=jax.ShapeDtypeStruct((frames * channels * out_rows, half), bf16),
         scratch_shapes=[
-            pltpu.VMEM((3 * own.shape[0], width), bf16),
             pltpu.VMEM((frames + 4, len(apart) * depth, half), bf16),
             pltpu.VMEM((frames + 2, (rows + 3) * VIEWS * channels, half), bf16),
             pltpu.VMEM((frames, (rows + 3) * pair, half), bf16),

time: 11.6 us -> 11.6 us (level)
  no operation moved by 1% of the time
where the time goes in v10:
time: 11.6 us; the launch traced here: 11.5 us
  Pallas kernels  5.72 us (49%)
  starting transfers between devices  3.32 us (29%)
  waiting for transfers between devices  1.69 us (15%)
  between operations  0.72 us (6%)
    pallas_call x1, Pallas kernels, shards(): pl.pallas_call(lambda *refs: encode_kernel(*refs, rows=rows, frames=frame...  2.87 us
    ppermute x1, starting transfers between devices, shards(): there = lax.ppermute(own, axes, route)  2.82 us
    pallas_call x1, Pallas kernels, shards(): pl.pallas_call(lambda *refs: prepare_kernel(*refs, rows=rows, frames=fram...  1.73 us
    ppermute x1, waiting for transfers between devices, shards(): back = lax.ppermute(own, axes, [(b, a) for a, b in route])  1.69 us
    pallas_call x1, Pallas kernels, shards(): pl.pallas_call(lambda *refs: load_kernel(*refs, rows=rows, frames=frames)...  1.11 us
    ppermute x1, starting transfers between devices, shards(): lax.ppermute(pixels[0, -4:], 'frames', [(i, (i + 1) % frame_devices) for...  0.49 us
  transfers between devices with their start and end apart: 3, of which 1 were waited for; matrix products, arithmetic and copies ran while one was open for 0% of the time, Pallas kernels for 25%

profile of v10, /device:TPU:0, one launch (start us, length us, event | category | flops | bytes accessed | tf_op | source)
XLA Modules:
  0.0 11.5 jit_solution(16633578244205922085)
XLA Ops:
  0.0 0.5 %collective-permute-start = (bf16[4,3,4,256]{3,2,1,0:T(4,128)(2,1)}, bf16[4,3,4,256]{3,2,1,0:T(4,128)(2,1)S(1)}, u32[]{:S(2)}, u32[]{:S(2)}) collective-permute-start(bf16[4,3,4,256]{3,2,1,0:T(4,128)(2,1)} %bitcast.10), channel_id=1, source_target_pairs={{0,1},{1,0},{2,3},{3,2},{4,5},{5,4},{6,7},{7,6},{8,9},{9,8},{10,11... | collective-permute-start | bytes 73736 | tf_op jit(solution)/shard_map/ppermute | solution.py:304
  0.5 1.1 %load.1 = (bf16[4,3,4,256]{3,2,1,0:T(4,128)(2,1)S(1)}, bf16[27,3,64]{2,1,0:T(4,128)(2,1)S(1)}, bf16[27,64,64]{2,1,0:T(8,128)(2,1)S(1)}, bf16[9,64,64]{2,1,0:T(8,...) custom-call(bf16[4,3,4,256]{3,2,1,0:T(4,128)(2,1)} %bitcast.11, ...), custom_call_target="tpu_custom_call" | custom-call | tf_op jit(solution)/shard_map/load/pallas_call | solution.py:320
  1.6 0.0 collective-permute-done
  1.7 2.8 %collective-permute-start.1 = (bf16[96,256]{1,0:T(8,128)(2,1)S(1)}, bf16[96,256]{1,0:T(8,128)(2,1)S(1)}, u32[]{:S(2)}, u32[]{:S(2)}) collective-permute-start(bf16[96,256]{1,0:T(8,128)(2,1)S(1)} %pad_maximum_fusion.refs_1_.refs_0_), channel_id=1, source_target_pairs={{0,4},{4,8},{8,12},{12,13},{13,9},{9,5},{5,1},{1,0},{2,6},{6,10},{... | collective-permute-start | bytes 147464 | tf_op jit(solution)/shard_map/ppermute | solution.py:337
  4.5 0.0 collective-permute-start.2
  5.2 1.7 %prepare.1 = (bf16[384,192]{1,0:T(8,128)(2,1)S(1)}, bf16[128,2304]{1,0:T(8,128)(2,1)S(1)}, bf16[128,960]{1,0:T(8,128)(2,1)S(1)}, f32[7,768]{1,0:T(8,128)S(1)}, b...) custom-call(s32[1]{0:T(128)S(6)} %copy.6.refs_0_, bf16[96,256]{1,0:T(8,128)(2,1)S(1)} %pad_maximum_fusion.refs_1_.refs_0_, ...), custom_call_target="tpu_custom_call" | custom-call | tf_op jit(solution)/shard_map/prepare/pallas_call | solution.py:342
  6.9 0.0 collective-permute-done.1.refs_1_
  6.9 1.7 %collective-permute-done.2.refs_2_ = bf16[96,256]{1,0:T(8,128)(2,1)S(1)} collective-permute-done((bf16[96,256]{1,0:T(8,128)(2,1)S(1)}, bf16[96,256]{1,0:T(8,128)(2,1)S(1)}, u32[]{:S(2)}, u32[]{:S(2)}) %collective-permute-start.2) | collective-permute-done | bytes 49184 | tf_op jit(solution)/shard_map/ppermute | solution.py:336
  8.6 2.9 %encode.1 = bf16[512,128]{1,0:T(8,128)(2,1)} custom-call(bf16[96,256]{1,0:T(8,128)(2,1)S(1)} %pad_maximum_fusion.refs_1_.refs_0_, bf16[96,256]{1,0:T(8,128)(2,1)S(1)} %collective-permute-done.1.refs_1_, bf16[96,256]{1,0:T(8,128)(2,1)S(1)} %collective-permute-done.2.refs_2_, bf16[128,144]{1,0:T(8,128)(2,1)S(1)} %get-tuple-element.23.refs_3_, ...), custom_call_target="tpu_custom_call" | custom-call | tf_op jit(solution)/shard_map/encode/pallas_call | solution.py:361
  (4 shorter events, 0.0 us)
Async XLA Ops:
  0.0 1.6 %collective-permute-start = (bf16[4,3,4,256]{3,2,1,0:T(4,128)(2,1)}, bf16[4,3,4,256]{3,2,1,0:T(4,128)(2,1)S(1)}, u32[]{:S(2)}, u32[]{:S(2)}) collective-permute-start(bf16[4,3,4,256]{3,2,1,0:T(4,128)(2,1)} %bitcast.10), channel_id=1, source_target_pairs={{0,1},{1,0},{2,3},{3,2},{4,5},{5,4},{6,7},{7,6},{8,9},{9,8},{10,11... | collective-permute-start | bytes 73736 | tf_op jit(solution)/shard_map/ppermute | solution.py:304
  1.7 5.2 %collective-permute-start.1 = (bf16[96,256]{1,0:T(8,128)(2,1)S(1)}, bf16[96,256]{1,0:T(8,128)(2,1)S(1)}, u32[]{:S(2)}, u32[]{:S(2)}) collective-permute-start(bf16[96,256]{1,0:T(8,128)(2,1)S(1)} %pad_maximum_fusion.refs_1_.refs_0_), channel_id=1, source_target_pairs={{0,4},{4,8},{8,12},{12,13},{13,9},{9,5},{5,1},{1,0},{2,6},{6,10},{... | collective-permute-start | bytes 147464 | tf_op jit(solution)/shard_map/ppermute | solution.py:337
  4.5 4.1 %collective-permute-start.2 = (bf16[96,256]{1,0:T(8,128)(2,1)S(1)}, bf16[96,256]{1,0:T(8,128)(2,1)S(1)}, u32[]{:S(2)}, u32[]{:S(2)}) collective-permute-start(bf16[96,256]{1,0:T(8,128)(2,1)S(1)} %pad_maximum_fusion.refs_1_.refs_0_), channel_id=1, source_target_pairs={{4,0},{8,4},{12,8},{13,12},{9,13},{5,9},{1,5},{0,1},{6,2},{10,6},{... | collective-permute-start | bytes 147464 | tf_op jit(solution)/shard_map/ppermute | solution.py:336
